TPU v7x, 32 devices: a whole 2x2x4 slice. The times are simulated.
32 devices in a mesh: wide: 4 (over z), grp: 4 (over y, x), rep: 2 (over core).
Axes of the slice: x: 2, y: 2, z: 4, core: 2. Of those that a mesh axis runs over, the one named last changes fastest.
Arguments:
- hidden_in: bfloat16 [1024, 2048], P(('wide', 'rep'), 'grp'), may hold values from -6 to 6
- grad_out: bfloat16 [1024, 2048], P(('wide', 'rep'), 'grp'), may hold values from -6 to 6
- route_ids: int32 [1024, 8], P(('wide', 'rep')), may hold values from 0 to 15, all different within a row; in each aligned block of 128 rows (0 to 127, 128 to 255, ...) at most 96 rows name the same one
- route_weights: float32 [1024, 8], P(('wide', 'rep')), may hold values from 0.05 to 1
- gate_proj: bfloat16 [16, 2048, 768], P('wide', None, 'rep'), may hold values from -0.125 to 0.125
- up_proj: bfloat16 [16, 2048, 768], P('wide', None, 'rep'), may hold values from -0.125 to 0.125
- down_proj: bfloat16 [16, 768, 2048], P('wide', 'rep'), may hold values from -0.21875 to 0.21875
Outputs:
- grad_in: bfloat16 [1024, 2048], P(('wide', 'rep'), 'grp')
Inputs may be any that keep to these rules, and one draw needn't show every extreme that they name: `route_ids`: each row names 8 different experts. In each aligned block of 128 rows (the rows of one index of wide+rep) no expert is named by more than 96 rows, a bound that some block reaches.
All inputs are finite; a program needn't handle non-finite values.
Results may differ from a plain program's by a relative error of at most 0.0064.
Values may be sent and summed in bfloat16 or wider, within the bound.
No kernel may reach another device: no remote copies, remote signals or barrier semaphores. Data moves between devices by JAX's collectives and lax.ppermute only.
A program may use at most 128 MiB of HBM per device.

v0:
```python
import jax
import jax.numpy as jnp
from jax import lax
from jax.experimental import pallas as pl
from jax.experimental.pallas import tpu as pltpu
from jax.sharding import PartitionSpec as P


def expert_back(stacked, gate_mat, up_mat, down_mat):
    inputs = stacked[0]
    scaled = stacked[1]
    pre_gate = jnp.einsum("wecd,edf->wecf", inputs, gate_mat, preferred_element_type=jnp.float32)
    pre_up = jnp.einsum("wecd,edf->wecf", inputs, up_mat, preferred_element_type=jnp.float32)
    back_hidden = jnp.einsum("wecd,efd->wecf", scaled, down_mat, preferred_element_type=jnp.float32)
    gate_sig = jax.nn.sigmoid(pre_gate)
    d_gate = (back_hidden * pre_up * gate_sig * (1.0 + pre_gate * (1.0 - gate_sig))).astype(
        jnp.bfloat16
    )
    d_up = (back_hidden * pre_gate * gate_sig).astype(jnp.bfloat16)
    first_term = jnp.einsum("wecf,edf->wecd", d_gate, gate_mat, preferred_element_type=jnp.float32)
    return first_term + jnp.einsum(
        "wecf,edf->wecd", d_up, up_mat, preferred_element_type=jnp.float32
    )


def slot_ranks(pair_ids, experts):
    pairs = pair_ids.shape[0]
    block = 128
    nblocks = pairs // block
    onehot = (pair_ids[:, None] == jnp.arange(experts, dtype=jnp.int32)[None, :]).astype(
        jnp.bfloat16
    )
    onehot = onehot.reshape(nblocks, block, experts)
    lower = (
        lax.broadcasted_iota(jnp.int32, (block, block), 0)
        > lax.broadcasted_iota(jnp.int32, (block, block), 1)
    ).astype(jnp.bfloat16)
    within = jnp.einsum("ij,bje->bie", lower, onehot, preferred_element_type=jnp.float32)
    totals = jnp.sum(onehot.astype(jnp.float32), axis=1)
    before = jnp.cumsum(totals, axis=0) - totals
    counted = jnp.sum((within + before[:, None, :]) * onehot.astype(jnp.float32), axis=2)
    return counted.reshape(pairs).astype(jnp.int32)


def routed_shards(hidden_in, grad_out, route_ids, route_weights, gate_proj, up_proj, down_proj):
    tok_rows, local_cols = hidden_in.shape
    fanout = route_ids.shape[1]
    wide_size = lax.axis_size("wide")
    groups = lax.axis_size("grp")
    local_experts = gate_proj.shape[0]
    experts = local_experts * wide_size
    capacity = groups * max(1, 3 * tok_rows * fanout // (2 * experts * groups))
    pair_ids = route_ids.reshape(-1)
    slot_rank = slot_ranks(pair_ids, experts)
    position = pair_ids * capacity + slot_rank
    token_ids = jnp.arange(tok_rows * fanout, dtype=jnp.int32) // fanout
    pair_inputs = hidden_in[token_ids]
    pair_scaled = (
        route_weights.reshape(-1)[:, None] * grad_out[token_ids].astype(jnp.float32)
    ).astype(jnp.bfloat16)
    blank_rows = jnp.zeros((experts * capacity, local_cols), jnp.bfloat16)
    outgoing = jnp.stack(
        [blank_rows.at[position].set(pair_inputs), blank_rows.at[position].set(pair_scaled)]
    )
    outgoing = outgoing.reshape(2, wide_size, local_experts, capacity, local_cols)
    received = lax.all_to_all(
        lax.all_to_all(outgoing, "wide", split_axis=1, concat_axis=1, tiled=True),
        "grp",
        split_axis=3,
        concat_axis=4,
        tiled=True,
    )
    full_gate, full_up, full_down = (
        lax.all_gather(gate_proj, "rep", axis=2, tiled=True),
        lax.all_gather(up_proj, "rep", axis=2, tiled=True),
        lax.all_gather(down_proj, "rep", axis=1, tiled=True),
    )
    summed = expert_back(received, full_gate, full_up, full_down)
    returned = lax.all_to_all(
        lax.all_to_all(
            summed.astype(jnp.bfloat16), "wide", split_axis=0, concat_axis=0, tiled=True
        ),
        "grp",
        split_axis=3,
        concat_axis=2,
        tiled=True,
    )
    flat_rows = returned.reshape(experts * capacity, local_cols)
    picked = flat_rows[position].astype(jnp.float32).reshape(tok_rows, fanout, local_cols)
    return jnp.sum(picked, axis=1).astype(jnp.bfloat16)


LANES = 128
VMEM = pl.BlockSpec(memory_space=pltpu.VMEM)
SMEM = pl.BlockSpec(memory_space=pltpu.SMEM)
HBM = pl.BlockSpec(memory_space=pltpu.HBM)


def load_kernel(gate_hbm, up_hbm, down_hbm, after, scalars, both, both_t, down_t, down, sems):
    local, _, half = gate_hbm.shape
    copies = []
    for e in range(local):
        copies.append(
            (
                pltpu.make_async_copy(gate_hbm.at[e], both.at[e, :, :half], sems.at[e, 0]),
                pltpu.make_async_copy(up_hbm.at[e], both.at[e, :, half:], sems.at[e, 1]),
                pltpu.make_async_copy(down_hbm.at[e], down.at[e], sems.at[e, 2]),
            )
        )
        for copy in copies[e]:
            copy.start()
    for e in range(local):
        for copy in copies[e]:
            copy.wait()
        both_t[e] = both[e].T
        down_t[:, e * half : (e + 1) * half] = down[e].T


def load_weights(gate_proj, up_proj, down_proj, after, scalars):
    local, width, half = gate_proj.shape
    size = 6 * local * width * half
    weights = [pltpu.with_memory_space_constraint(w, pltpu.HBM) for w in (gate_proj, up_proj, down_proj)]
    return pl.pallas_call(
        load_kernel,
        in_specs=[HBM] * 3 + [VMEM, SMEM],
        out_specs=[VMEM] * 3,
        out_shape=[
            jax.ShapeDtypeStruct((local, width, 2 * half), jnp.bfloat16),
            jax.ShapeDtypeStruct((local, 2 * half, width), jnp.bfloat16),
            jax.ShapeDtypeStruct((width, local * half), jnp.bfloat16),
        ],
        scratch_shapes=[
            pltpu.VMEM(down_proj.shape, jnp.bfloat16),
            pltpu.SemaphoreType.DMA((local, 3)),
        ],
        compiler_params=pltpu.CompilerParams(vmem_limit_bytes=8 << 20),
        cost_estimate=pl.CostEstimate(flops=0, bytes_accessed=size, transcendentals=0),
        name="load",
    )(*weights, after, scalars)


def chunk_kernel(groups, count, scalars, *refs):
    place, wide = scalars[0], scalars[1]
    blocks = refs[:count]
    both, both_t, down_t, mine_out, other_out, x_rows, g_rows, total = refs[count:]
    local, width, double = both.shape
    half = double // 2
    height = blocks[0].shape[0]
    cols = width // groups
    for number, block in enumerate(blocks):
        rows = slice(number * height, (number + 1) * height)
        for step in range(groups):
            start = pl.multiple_of((place ^ step) * cols, LANES)
            x_rows[rows, pl.ds(start, cols)] = block[:, 2 * step * cols : (2 * step + 1) * cols]
            g_rows[rows, pl.ds(start, cols)] = block[:, (2 * step + 1) * cols : (2 * step + 2) * cols]
    weights = jnp.concatenate([block[:, 2 * width :] for block in blocks], axis=0)
    weights = weights.astype(jnp.float32)
    lane = lax.broadcasted_iota(jnp.int32, weights.shape, 1)
    experts = weights.shape[1] // 2

    for e in range(local):
        named = (lane == wide * local + e) | (lane == wide * local + e + experts)
        route = jnp.sum(jnp.where(named, weights, 0.0), axis=1, keepdims=True)
        pre = jnp.dot(x_rows[...], both[e], preferred_element_type=jnp.float32)
        if e % 2 == 0:
            paired = min(2, local - e)
            back_pair = jnp.dot(
                g_rows[...],
                down_t[:, e * half : (e + paired) * half],
                preferred_element_type=jnp.float32,
            )
        back = route * back_pair[:, (e % 2) * half : (e % 2 + 1) * half]
        pre_gate, pre_up = pre[:, :half], pre[:, half:]
        sig = 1.0 / (1.0 + jnp.exp(-pre_gate))
        d_gate = back * pre_up * sig * (1.0 + pre_gate * (1.0 - sig))
        d_up = back * pre_gate * sig
        hidden = jnp.concatenate([d_gate, d_up], axis=1).astype(jnp.bfloat16)
        term = jnp.dot(hidden, both_t[e], preferred_element_type=jnp.float32)
        if e == 0:
            total[...] = term
        else:
            total[...] += term
    for number in range(count):
        rows = slice(number * height, (number + 1) * height)
        out = mine_out if number < count // 2 else other_out
        for step in range(groups):
            start = pl.multiple_of((place ^ step) * cols, LANES)
            part = total[rows, pl.ds(start, cols)]
            out[number % (count // 2), :, step * cols : (step + 1) * cols] = part.astype(out.dtype)


def chunk_gradient(scalars, mine, other, weights, groups):
    local, width, double = weights[0].shape
    slots, height = len(mine), mine[0].shape[0]
    rows = 2 * slots * height
    return pl.pallas_call(
        lambda *refs: chunk_kernel(groups, 2 * slots, *refs),
        in_specs=[SMEM] + [VMEM] * (2 * slots + 3),
        out_specs=[VMEM, VMEM],
        out_shape=[
            jax.ShapeDtypeStruct((slots, height, width), jnp.float32),
            jax.ShapeDtypeStruct((slots, height, width), jnp.bfloat16),
        ],
        scratch_shapes=[
            pltpu.VMEM((rows, width), jnp.bfloat16),
            pltpu.VMEM((rows, width), jnp.bfloat16),
            pltpu.VMEM((rows, width), jnp.float32),
        ],
        compiler_params=pltpu.CompilerParams(vmem_limit_bytes=16 * rows * width),
        cost_estimate=pl.CostEstimate(
            flops=10 * 256 * width * (double // 2) * local // 2,
            bytes_accessed=4 * rows * width,
            transcendentals=rows * (double // 2) * local,
        ),
        name="chunk",
    )(scalars, *mine, *other, *weights)


def join_kernel(mine, swapped, *outs):
    for number, out in enumerate(outs):
        out[...] = (mine[number] + swapped[number].astype(jnp.float32)).astype(out.dtype)


def join(mine, swapped, kinds):
    shape = mine.shape[1:]
    return pl.pallas_call(
        join_kernel,
        in_specs=[VMEM] * 2,
        out_specs=[VMEM] * len(kinds),
        out_shape=[jax.ShapeDtypeStruct(shape, kind) for kind in kinds],
        compiler_params=pltpu.CompilerParams(vmem_limit_bytes=1 << 20),
        name="join",
    )(mine, swapped)


def flip(array, axis, step):
    size = lax.axis_size(axis)
    return lax.ppermute(array, axis, [(i, i ^ step) for i in range(size)])


def route_table(route_ids, route_weights, experts):
    chosen = route_ids[:, :, None] == jnp.arange(experts, dtype=jnp.int32)[None, None, :]
    return jnp.sum(jnp.where(chosen, route_weights[:, :, None], 0.0), axis=1)


def gathered(block, axis):
    size = lax.axis_size(axis)
    parts = {0: block}
    step = size // 2
    while step:
        for k in sorted(parts):
            parts[k | step] = flip(parts[k], axis, step)
        step //= 2
    return [parts[k] for k in range(size)]


def dense_shards(hidden_in, grad_out, route_ids, route_weights, gate_proj, up_proj, down_proj):
    tok_rows, cols = hidden_in.shape
    wide_size = lax.axis_size("wide")
    groups = lax.axis_size("grp")
    local = gate_proj.shape[0]
    height = tok_rows // groups
    place = lax.axis_index("grp").astype(jnp.int32)
    wide = lax.axis_index("wide").astype(jnp.int32)
    scalars = jnp.stack([place, wide])

    pieces = []
    for step in range(groups):
        first = (place ^ step) * height
        piece = jnp.concatenate(
            [lax.dynamic_slice_in_dim(a, first, height, 0) for a in (hidden_in, grad_out)], axis=1
        )
        pieces.append(piece if step == 0 else flip(piece, "grp", step))
    ids = lax.dynamic_slice_in_dim(route_ids, place * height, height, 0)
    route = lax.dynamic_slice_in_dim(route_weights, place * height, height, 0)
    table = route_table(ids, route, local * wide_size)
    table = jnp.pad(table, ((0, 0), (0, LANES // 2 - table.shape[1])))
    high = table.astype(jnp.bfloat16)
    low = (table - high.astype(jnp.float32)).astype(jnp.bfloat16)
    block = jnp.concatenate(pieces + [high, low], axis=1)
    weights = load_weights(gate_proj, up_proj, down_proj, block, scalars)
    blocks = gathered(block, "wide")
    half_way = wide_size // 2
    order = [k for k in range(1, wide_size)] + [0]
    chunks = [order[i : i + half_way] for i in range(0, wide_size, half_way)] if half_way else [[0]]
    others = [flip(b, "rep", 1) for b in blocks]
    summed = jnp.zeros((height, cols * groups), jnp.float32)
    for chunk in chunks:
        mine, other = chunk_gradient(
            scalars, [blocks[k] for k in chunk], [others[k] for k in chunk], weights, groups
        )
        kinds = [jnp.bfloat16 if k else jnp.float32 for k in chunk]
        for k, part in zip(chunk, join(mine, flip(other, "rep", 1), kinds)):
            if k:
                part = flip(part, "wide", k)
                part = part.astype(jnp.float32)
            summed = summed + part
    summed = summed.astype(jnp.bfloat16)
    pieces = []
    for step in range(groups):
        piece = summed[:, step * cols : (step + 1) * cols]
        pieces.append(piece if step == 0 else flip(piece, "grp", step))
    bit = 1
    while bit < groups:
        swap = (place & bit) != 0
        pieces = [jnp.where(swap, pieces[k ^ bit], pieces[k]) for k in range(groups)]
        bit *= 2
    return jnp.concatenate(pieces, axis=0)


def shards(hidden_in, grad_out, route_ids, route_weights, gate_proj, up_proj, down_proj):
    wide_size, groups = lax.axis_size("wide"), lax.axis_size("grp")
    experts = gate_proj.shape[0] * wide_size
    fanout = route_ids.shape[1]
    powers = all(n & (n - 1) == 0 for n in (wide_size, groups))
    dense = powers and experts <= 2 * fanout and 2 * experts <= LANES and lax.axis_size("rep") == 2
    path = dense_shards if dense else routed_shards
    return path(
        hidden_in, grad_out, route_ids, route_weights, gate_proj, up_proj, down_proj
    )


def solution(mesh):
    in_specs = (
        P(("wide", "rep"), "grp"),
        P(("wide", "rep"), "grp"),
        P(("wide", "rep"), None),
        P(("wide", "rep"), None),
        P("wide", None, "rep"),
        P("wide", None, "rep"),
        P("wide", "rep", None),
    )
    out_specs = P(("wide", "rep"), "grp")
    return jax.shard_map(
        shards, mesh=mesh, in_specs=in_specs, out_specs=out_specs, check_vma=False
    )
```

profile of v0, /device:TPU:0, one launch (start us, length us, event | category | flops | bytes accessed | tf_op | source)
XLA Modules:
  0.0 68.0 jit_solution(9021876726469910984)
XLA Ops:
  0.0 0.0 copy-start
  0.0 0.9 %constant_dynamic-slice_fusion.2 = (bf16[32,512]{1,0:T(8,128)(2,1)S(1)}, bf16[32,512]{1,0:T(8,128)(2,1)S(1)}, bf16[32,512]{1,0:T(8,128)(2,1)S(1)}, bf16[32,512]{...) fusion(bf16[128,512]{1,0:T(8,128)(2,1)} %param.8, ...), kind=kLoop, calls=%fused_computation.19 | loop fusion | bytes 524304 | tf_op jit(solution)/shard_map/dynamic_slice | solution.py:271
  0.9 4.0 %collective-permute-start.2 = (bf16[32,1024]{1,0:T(8,128)(2,1)S(1)}, bf16[32,1024]{1,0:T(8,128)(2,1)S(1)}, u32[]{:S(2)}, u32[]{:S(2)}) collective-permute-start(bf16[32,1024]{1,0:T(8,128)(2,1)S(1)} %pad_maximum_fusion.3), channel_id=1, source_target_pairs={{0,6},{2,4},{4,2},{6,0},{1,7},{3,5},{5,3},{7,1},{8,14},{10,12},{12... | collective-permute-start | bytes 196616 | tf_op jit(solution)/shard_map/ppermute | solution.py:238
  4.9 0.5 collective-permute-start.1
  5.4 0.1 collective-permute-start
  5.6 0.0 copy-done
  5.6 0.1 constant_dynamic-slice_fusion
  5.6 0.8 %constant_dynamic-slice_fusion.1 = s32[32,8]{0,1:T(8,128)S(1)} fusion(s32[128,8]{0,1:T(8,128)} %param.9, s32[]{:T(128)S(6)} %select_n.62), kind=kLoop, calls=%fused_computation.18 | loop fusion | bytes 2052 | tf_op jit(solution)/shard_map/dynamic_slice | solution.py:274
  6.4 0.1 copy.10
  6.5 0.6 collective-permute-done.2
  7.2 2.0 %collective-permute-done.1 = bf16[32,1024]{1,0:T(8,128)(2,1)S(1)} collective-permute-done((bf16[32,1024]{1,0:T(8,128)(2,1)S(1)}, bf16[32,1024]{1,0:T(8,128)(2,1)S(1)}, u32[]{:S(2)}, u32[]{:S(2)}) %collective-permute-start.1) | collective-permute-done | bytes 65568 | tf_op jit(solution)/shard_map/ppermute | solution.py:238
  9.2 0.5 collective-permute-done
  9.7 0.1 concatenate.18.after.refs_2_
  9.8 2.6 %collective-permute-start.4 = (bf16[32,4224]{1,0:T(8,128)(2,1)S(1)}, bf16[32,4224]{1,0:T(8,128)(2,1)S(1)}, u32[]{:S(2)}, u32[]{:S(2)}) collective-permute-start(bf16[32,4224]{1,0:T(8,128)(2,1)S(1)} %concatenate.18.after.refs_2_), channel_id=1, source_target_pairs={{0,16},{8,24},{16,0},{24,8},{1,17},{9,25},{17,1},{25,9},{2,18},{10... | collective-permute-start | bytes 811016 | tf_op jit(solution)/shard_map/ppermute | solution.py:238
  12.4 1.6 %collective-permute-start.3 = (bf16[32,4224]{1,0:T(8,128)(2,1)S(1)}, bf16[32,4224]{1,0:T(8,128)(2,1)S(1)}, u32[]{:S(2)}, u32[]{:S(2)}) collective-permute-start(bf16[32,4224]{1,0:T(8,128)(2,1)S(1)} %concatenate.18.after.refs_2_), channel_id=1, source_target_pairs={{0,8},{8,0},{16,24},{24,16},{1,9},{9,1},{17,25},{25,17},{2,10},{10... | collective-permute-start | bytes 811016 | tf_op jit(solution)/shard_map/ppermute | solution.py:238
  14.0 9.5 %collective-permute-done.4.refs_2_ = bf16[32,4224]{1,0:T(8,128)(2,1)S(1)} collective-permute-done((bf16[32,4224]{1,0:T(8,128)(2,1)S(1)}, bf16[32,4224]{1,0:T(8,128)(2,1)S(1)}, u32[]{:S(2)}, u32[]{:S(2)}) %collective-permute-start.4) | collective-permute-done | bytes 270368 | tf_op jit(solution)/shard_map/ppermute | solution.py:238
  23.5 0.6 collective-permute-start.10
  24.1 0.0 collective-permute-done.3.refs_1_
  24.1 0.0 collective-permute-start.5
  24.1 0.5 collective-permute-start.6
  24.6 0.1 pad_add_fusion.scalars.refs_0_
  24.7 0.0 collective-permute-start.12
  24.7 8.4 %load.1 = (bf16[4,2048,768]{2,1,0:T(8,128)(2,1)S(1)}, bf16[4,768,2048]{2,1,0:T(8,128)(2,1)S(1)}, bf16[2048,1536]{1,0:T(8,128)(2,1)S(1)}) custom-call(bf16[4,2048,384]{2,1,0:T(8,128)(2,1)} %gate_hbm.1, bf16[4,2048,384]{2,1,0:T(8,128)(2,1)} %up_hbm.1, bf16[4,384,2048]{2,1,0:T(8,128)(2,1)} %down_hbm.1, bf16[32,4224]{1,0:T(8,128)(2,1)S(1)} %concatenate.18.after.refs_2_, ...), custom_call_target="tpu_custom_call" | custom-call | bytes 18874368 | tf_op jit(solution)/shard_map/load/pallas_call | solution.py:123
  33.1 0.0 collective-permute-done.10.refs_1_
  33.2 0.6 collective-permute-start.11
  33.7 0.0 collective-permute-done.5.refs_3_
  33.7 0.0 collective-permute-done.6.refs_4_
  33.7 5.8 %chunk.2 = (f32[2,32,2048]{2,1,0:T(8,128)S(1)}, bf16[2,32,2048]{2,1,0:T(8,128)(2,1)S(1)}) custom-call(s32[2]{0:T(128)S(1)} %pad_add_fusion.scalars.refs_0_, bf16[32,4224]{1,0:T(8,128)(2,1)S(1)} %collective-permute-done.3.refs_1_, bf16[32,4224]{1,0:T(8,128)(2,1)S(1)} %collective-permute-done.4.refs_2_, bf16[32,4224]{1,0:T(8,128)(2,1)S(1)} %collective-permute-done.5.refs_3_, ...), custom_call_target="tpu_custom_call" | custom-call | flops 4026531840 | bytes 1048576 | tf_op jit(solution)/shard_map/chunk/pallas_call | solution.py:196
  39.6 0.1 collective-permute-start.7
  39.7 0.0 collective-permute-done.12.refs_4_
  39.7 0.0 collective-permute-done.11.refs_3_
  39.7 6.0 %chunk.3 = (f32[2,32,2048]{2,1,0:T(8,128)S(1)}, bf16[2,32,2048]{2,1,0:T(8,128)(2,1)S(1)}) custom-call(s32[2]{0:T(128)S(1)} %pad_add_fusion.scalars.refs_0_, bf16[32,4224]{1,0:T(8,128)(2,1)S(1)} %collective-permute-done.10.refs_1_, bf16[32,4224]{1,0:T(8,128)(2,1)S(1)} %concatenate.18.after.refs_2_, bf16[32,4224]{1,0:T(8,128)(2,1)S(1)} %collective-permute-done.11.refs_3_, ...), custom_call_target="tpu_custom_call" | custom-call | flops 4026531840 | bytes 1048576 | tf_op jit(solution)/shard_map/chunk/pallas_call | solution.py:196
  45.7 0.6 collective-permute-start.13
  46.3 0.0 collective-permute-done.7.swapped
  46.3 0.1 join.2
  46.3 1.5 %collective-permute-start.8 = (bf16[32,2048]{1,0:T(8,128)(2,1)S(1)}, bf16[32,2048]{1,0:T(8,128)(2,1)S(1)}, u32[]{:S(2)}, u32[]{:S(2)}) collective-permute-start(bf16[32,2048]{1,0:T(8,128)(2,1)S(1)} %get-tuple-element.21), channel_id=1, source_target_pairs={{0,8},{8,0},{16,24},{24,16},{1,9},{9,1},{17,25},{25,17},{2,10},{10... | collective-permute-start | bytes 393224 | tf_op jit(solution)/shard_map/ppermute | solution.py:238
  47.9 2.0 %collective-permute-start.9 = (bf16[32,2048]{1,0:T(8,128)(2,1)S(1)}, bf16[32,2048]{1,0:T(8,128)(2,1)S(1)}, u32[]{:S(2)}, u32[]{:S(2)}) collective-permute-start(bf16[32,2048]{1,0:T(8,128)(2,1)S(1)} %get-tuple-element.22), channel_id=1, source_target_pairs={{0,16},{8,24},{16,0},{24,8},{1,17},{9,25},{17,1},{25,9},{2,18},{10... | collective-permute-start | bytes 393224 | tf_op jit(solution)/shard_map/ppermute | solution.py:238
  49.9 0.0 collective-permute-done.13.swapped
  49.9 1.5 %collective-permute-start.14 = (bf16[32,2048]{1,0:T(8,128)(2,1)S(1)}, bf16[32,2048]{1,0:T(8,128)(2,1)S(1)}, u32[]{:S(2)}, u32[]{:S(2)}) collective-permute-start(bf16[32,2048]{1,0:T(8,128)(2,1)S(1)} %get-tuple-element.25), channel_id=1, source_target_pairs={{0,24},{8,16},{16,8},{24,0},{1,25},{9,17},{17,9},{25,1},{2,26},{10... | collective-permute-start | bytes 393224 | tf_op jit(solution)/shard_map/ppermute | solution.py:238
  51.4 3.1 %collective-permute-done.8 = bf16[32,2048]{1,0:T(8,128)(2,1)S(1)} collective-permute-done((bf16[32,2048]{1,0:T(8,128)(2,1)S(1)}, bf16[32,2048]{1,0:T(8,128)(2,1)S(1)}, u32[]{:S(2)}, u32[]{:S(2)}) %collective-permute-start.8) | collective-permute-done | bytes 131104 | tf_op jit(solution)/shard_map/ppermute | solution.py:238
  54.4 0.8 %collective-permute-done.9 = bf16[32,2048]{1,0:T(8,128)(2,1)S(1)} collective-permute-done((bf16[32,2048]{1,0:T(8,128)(2,1)S(1)}, bf16[32,2048]{1,0:T(8,128)(2,1)S(1)}, u32[]{:S(2)}, u32[]{:S(2)}) %collective-permute-start.9) | collective-permute-done | bytes 131104 | tf_op jit(solution)/shard_map/ppermute | solution.py:238
  55.2 5.1 %collective-permute-done.14 = bf16[32,2048]{1,0:T(8,128)(2,1)S(1)} collective-permute-done((bf16[32,2048]{1,0:T(8,128)(2,1)S(1)}, bf16[32,2048]{1,0:T(8,128)(2,1)S(1)}, u32[]{:S(2)}, u32[]{:S(2)}) %collective-permute-start.14) | collective-permute-done | bytes 131104 | tf_op jit(solution)/shard_map/ppermute | solution.py:238
  60.4 0.1 add_convert_fusion
  60.4 1.8 %collective-permute-start.15 = (bf16[32,512]{1,0:T(8,128)(2,1)S(1)}, bf16[32,512]{1,0:T(8,128)(2,1)S(1)}, u32[]{:S(2)}, u32[]{:S(2)}) collective-permute-start(bf16[32,512]{1,0:T(8,128)(2,1)S(1)} %get-tuple-element.33), channel_id=1, source_target_pairs={{0,6},{2,4},{4,2},{6,0},{1,7},{3,5},{5,3},{7,1},{8,14},{10,12},{12... | collective-permute-start | bytes 98312 | tf_op jit(solution)/shard_map/ppermute | solution.py:238
  62.2 1.2 %collective-permute-start.16 = (bf16[32,512]{1,0:T(8,128)(2,1)S(1)}, bf16[32,512]{1,0:T(8,128)(2,1)S(1)}, u32[]{:S(2)}, u32[]{:S(2)}) collective-permute-start(bf16[32,512]{1,0:T(8,128)(2,1)S(1)} %get-tuple-element.32), channel_id=1, source_target_pairs={{0,4},{2,6},{4,0},{6,2},{1,5},{3,7},{5,1},{7,3},{8,12},{10,14},{12... | collective-permute-start | bytes 98312 | tf_op jit(solution)/shard_map/ppermute | solution.py:238
  63.4 0.6 collective-permute-start.17
  64.0 1.5 %collective-permute-done.15 = bf16[32,512]{1,0:T(8,128)(2,1)S(1)} collective-permute-done((bf16[32,512]{1,0:T(8,128)(2,1)S(1)}, bf16[32,512]{1,0:T(8,128)(2,1)S(1)}, u32[]{:S(2)}, u32[]{:S(2)}) %collective-permute-start.15) | collective-permute-done | bytes 32800 | tf_op jit(solution)/shard_map/ppermute | solution.py:238
  65.5 0.6 collective-permute-done.16
  66.2 1.2 %collective-permute-done.17 = bf16[32,512]{1,0:T(8,128)(2,1)S(1)} collective-permute-done((bf16[32,512]{1,0:T(8,128)(2,1)S(1)}, bf16[32,512]{1,0:T(8,128)(2,1)S(1)}, u32[]{:S(2)}, u32[]{:S(2)}) %collective-permute-start.17) | collective-permute-done | bytes 32800 | tf_op jit(solution)/shard_map/ppermute | solution.py:238
  67.4 0.7 pad_maximum_fusion
  (9 shorter events, 0.1 us)
Async XLA Ops:
  0.0 5.6 %copy-start = (f32[128,8]{0,1:T(8,128)S(1)}, f32[128,8]{0,1:T(8,128)}, u32[]{:S(2)}) copy-start(f32[128,8]{0,1:T(8,128)} %param.10) | copy-start | bytes 12292
  0.9 6.2 %collective-permute-start.2 = (bf16[32,1024]{1,0:T(8,128)(2,1)S(1)}, bf16[32,1024]{1,0:T(8,128)(2,1)S(1)}, u32[]{:S(2)}, u32[]{:S(2)}) collective-permute-start(bf16[32,1024]{1,0:T(8,128)(2,1)S(1)} %pad_maximum_fusion.3), channel_id=1, source_target_pairs={{0,6},{2,4},{4,2},{6,0},{1,7},{3,5},{5,3},{7,1},{8,14},{10,12},{12... | collective-permute-start | bytes 196616 | tf_op jit(solution)/shard_map/ppermute | solution.py:238
  4.9 4.3 %collective-permute-start.1 = (bf16[32,1024]{1,0:T(8,128)(2,1)S(1)}, bf16[32,1024]{1,0:T(8,128)(2,1)S(1)}, u32[]{:S(2)}, u32[]{:S(2)}) collective-permute-start(bf16[32,1024]{1,0:T(8,128)(2,1)S(1)} %pad_maximum_fusion.2), channel_id=1, source_target_pairs={{0,4},{2,6},{4,0},{6,2},{1,5},{3,7},{5,1},{7,3},{8,12},{10,14},{12... | collective-permute-start | bytes 196616 | tf_op jit(solution)/shard_map/ppermute | solution.py:238
  5.4 4.3 %collective-permute-start = (bf16[32,1024]{1,0:T(8,128)(2,1)S(1)}, bf16[32,1024]{1,0:T(8,128)(2,1)S(1)}, u32[]{:S(2)}, u32[]{:S(2)}) collective-permute-start(bf16[32,1024]{1,0:T(8,128)(2,1)S(1)} %pad_maximum_fusion.1), channel_id=1, source_target_pairs={{0,2},{2,0},{4,6},{6,4},{1,3},{3,1},{5,7},{7,5},{8,10},{10,8},{12,... | collective-permute-start | bytes 196616 | tf_op jit(solution)/shard_map/ppermute | solution.py:238
  9.8 13.7 %collective-permute-start.4 = (bf16[32,4224]{1,0:T(8,128)(2,1)S(1)}, bf16[32,4224]{1,0:T(8,128)(2,1)S(1)}, u32[]{:S(2)}, u32[]{:S(2)}) collective-permute-start(bf16[32,4224]{1,0:T(8,128)(2,1)S(1)} %concatenate.18.after.refs_2_), channel_id=1, source_target_pairs={{0,16},{8,24},{16,0},{24,8},{1,17},{9,25},{17,1},{25,9},{2,18},{10... | collective-permute-start | bytes 811016 | tf_op jit(solution)/shard_map/ppermute | solution.py:238
  12.4 11.7 %collective-permute-start.3 = (bf16[32,4224]{1,0:T(8,128)(2,1)S(1)}, bf16[32,4224]{1,0:T(8,128)(2,1)S(1)}, u32[]{:S(2)}, u32[]{:S(2)}) collective-permute-start(bf16[32,4224]{1,0:T(8,128)(2,1)S(1)} %concatenate.18.after.refs_2_), channel_id=1, source_target_pairs={{0,8},{8,0},{16,24},{24,16},{1,9},{9,1},{17,25},{25,17},{2,10},{10... | collective-permute-start | bytes 811016 | tf_op jit(solution)/shard_map/ppermute | solution.py:238
  23.5 9.6 %collective-permute-start.10 = (bf16[32,4224]{1,0:T(8,128)(2,1)S(1)}, bf16[32,4224]{1,0:T(8,128)(2,1)S(1)}, u32[]{:S(2)}, u32[]{:S(2)}) collective-permute-start(bf16[32,4224]{1,0:T(8,128)(2,1)S(1)} %collective-permute-done.4.refs_2_), channel_id=1, source_target_pairs={{0,8},{8,0},{16,24},{24,16},{1,9},{9,1},{17,25},{25,17},{2,10},{10... | collective-permute-start | bytes 811016 | tf_op jit(solution)/shard_map/ppermute | solution.py:238
  24.1 9.6 %collective-permute-start.5 = (bf16[32,4224]{1,0:T(8,128)(2,1)S(1)}, bf16[32,4224]{1,0:T(8,128)(2,1)S(1)}, u32[]{:S(2)}, u32[]{:S(2)}) collective-permute-start(bf16[32,4224]{1,0:T(8,128)(2,1)S(1)} %collective-permute-done.3.refs_1_), channel_id=1, source_target_pairs={{0,1},{1,0},{2,3},{3,2},{4,5},{5,4},{6,7},{7,6},{8,9},{9,8},{10,11... | collective-permute-start | bytes 811016 | tf_op jit(solution)/shard_map/ppermute | solution.py:238
  24.1 9.6 %collective-permute-start.6 = (bf16[32,4224]{1,0:T(8,128)(2,1)S(1)}, bf16[32,4224]{1,0:T(8,128)(2,1)S(1)}, u32[]{:S(2)}, u32[]{:S(2)}) collective-permute-start(bf16[32,4224]{1,0:T(8,128)(2,1)S(1)} %collective-permute-done.4.refs_2_), channel_id=1, source_target_pairs={{0,1},{1,0},{2,3},{3,2},{4,5},{5,4},{6,7},{7,6},{8,9},{9,8},{10,11... | collective-permute-start | bytes 811016 | tf_op jit(solution)/shard_map/ppermute | solution.py:238
  24.7 15.0 %collective-permute-start.12 = (bf16[32,4224]{1,0:T(8,128)(2,1)S(1)}, bf16[32,4224]{1,0:T(8,128)(2,1)S(1)}, u32[]{:S(2)}, u32[]{:S(2)}) collective-permute-start(bf16[32,4224]{1,0:T(8,128)(2,1)S(1)} %concatenate.18.after.refs_2_), channel_id=1, source_target_pairs={{0,1},{1,0},{2,3},{3,2},{4,5},{5,4},{6,7},{7,6},{8,9},{9,8},{10,11... | collective-permute-start | bytes 811016 | tf_op jit(solution)/shard_map/ppermute | solution.py:238
  33.2 6.5 %collective-permute-start.11 = (bf16[32,4224]{1,0:T(8,128)(2,1)S(1)}, bf16[32,4224]{1,0:T(8,128)(2,1)S(1)}, u32[]{:S(2)}, u32[]{:S(2)}) collective-permute-start(bf16[32,4224]{1,0:T(8,128)(2,1)S(1)} %collective-permute-done.10.refs_1_), channel_id=1, source_target_pairs={{0,1},{1,0},{2,3},{3,2},{4,5},{5,4},{6,7},{7,6},{8,9},{9,8},{10,11... | collective-permute-start | bytes 811016 | tf_op jit(solution)/shard_map/ppermute | solution.py:238
  39.6 6.7 %collective-permute-start.7 = (bf16[2,32,2048]{2,1,0:T(8,128)(2,1)S(1)}, bf16[2,32,2048]{2,1,0:T(8,128)(2,1)S(1)}, u32[]{:S(2)}, u32[]{:S(2)}) collective-permute-start(bf16[2,32,2048]{2,1,0:T(8,128)(2,1)S(1)} %get-tuple-element.20), channel_id=1, source_target_pairs={{0,1},{1,0},{2,3},{3,2},{4,5},{5,4},{6,7},{7,6},{8,9},{9,8},{10,11... | collective-permute-start | bytes 786440 | tf_op jit(solution)/shard_map/ppermute | solution.py:238
  45.7 4.1 %collective-permute-start.13 = (bf16[2,32,2048]{2,1,0:T(8,128)(2,1)S(1)}, bf16[2,32,2048]{2,1,0:T(8,128)(2,1)S(1)}, u32[]{:S(2)}, u32[]{:S(2)}) collective-permute-start(bf16[2,32,2048]{2,1,0:T(8,128)(2,1)S(1)} %get-tuple-element.24), channel_id=1, source_target_pairs={{0,1},{1,0},{2,3},{3,2},{4,5},{5,4},{6,7},{7,6},{8,9},{9,8},{10,11... | collective-permute-start | bytes 786440 | tf_op jit(solution)/shard_map/ppermute | solution.py:238
  46.3 8.1 %collective-permute-start.8 = (bf16[32,2048]{1,0:T(8,128)(2,1)S(1)}, bf16[32,2048]{1,0:T(8,128)(2,1)S(1)}, u32[]{:S(2)}, u32[]{:S(2)}) collective-permute-start(bf16[32,2048]{1,0:T(8,128)(2,1)S(1)} %get-tuple-element.21), channel_id=1, source_target_pairs={{0,8},{8,0},{16,24},{24,16},{1,9},{9,1},{17,25},{25,17},{2,10},{10... | collective-permute-start | bytes 393224 | tf_op jit(solution)/shard_map/ppermute | solution.py:238
  47.9 7.4 %collective-permute-start.9 = (bf16[32,2048]{1,0:T(8,128)(2,1)S(1)}, bf16[32,2048]{1,0:T(8,128)(2,1)S(1)}, u32[]{:S(2)}, u32[]{:S(2)}) collective-permute-start(bf16[32,2048]{1,0:T(8,128)(2,1)S(1)} %get-tuple-element.22), channel_id=1, source_target_pairs={{0,16},{8,24},{16,0},{24,8},{1,17},{9,25},{17,1},{25,9},{2,18},{10... | collective-permute-start | bytes 393224 | tf_op jit(solution)/shard_map/ppermute | solution.py:238
  49.9 10.5 %collective-permute-start.14 = (bf16[32,2048]{1,0:T(8,128)(2,1)S(1)}, bf16[32,2048]{1,0:T(8,128)(2,1)S(1)}, u32[]{:S(2)}, u32[]{:S(2)}) collective-permute-start(bf16[32,2048]{1,0:T(8,128)(2,1)S(1)} %get-tuple-element.25), channel_id=1, source_target_pairs={{0,24},{8,16},{16,8},{24,0},{1,25},{9,17},{17,9},{25,1},{2,26},{10... | collective-permute-start | bytes 393224 | tf_op jit(solution)/shard_map/ppermute | solution.py:238
  60.4 5.1 %collective-permute-start.15 = (bf16[32,512]{1,0:T(8,128)(2,1)S(1)}, bf16[32,512]{1,0:T(8,128)(2,1)S(1)}, u32[]{:S(2)}, u32[]{:S(2)}) collective-permute-start(bf16[32,512]{1,0:T(8,128)(2,1)S(1)} %get-tuple-element.33), channel_id=1, source_target_pairs={{0,6},{2,4},{4,2},{6,0},{1,7},{3,5},{5,3},{7,1},{8,14},{10,12},{12... | collective-permute-start | bytes 98312 | tf_op jit(solution)/shard_map/ppermute | solution.py:238
  62.2 3.9 %collective-permute-start.16 = (bf16[32,512]{1,0:T(8,128)(2,1)S(1)}, bf16[32,512]{1,0:T(8,128)(2,1)S(1)}, u32[]{:S(2)}, u32[]{:S(2)}) collective-permute-start(bf16[32,512]{1,0:T(8,128)(2,1)S(1)} %get-tuple-element.32), channel_id=1, source_target_pairs={{0,4},{2,6},{4,0},{6,2},{1,5},{3,7},{5,1},{7,3},{8,12},{10,14},{12... | collective-permute-start | bytes 98312 | tf_op jit(solution)/shard_map/ppermute | solution.py:238
  63.4 3.9 %collective-permute-start.17 = (bf16[32,512]{1,0:T(8,128)(2,1)S(1)}, bf16[32,512]{1,0:T(8,128)(2,1)S(1)}, u32[]{:S(2)}, u32[]{:S(2)}) collective-permute-start(bf16[32,512]{1,0:T(8,128)(2,1)S(1)} %get-tuple-element.31), channel_id=1, source_target_pairs={{0,2},{2,0},{4,6},{6,4},{1,3},{3,1},{5,7},{7,5},{8,10},{10,8},{12,... | collective-permute-start | bytes 98312 | tf_op jit(solution)/shard_map/ppermute | solution.py:238
where the time goes:
time: 68.5 us; the launch traced here: 68 us
  waiting for transfers between devices  25.1 us (37%)
  Pallas kernels  20.4 us (30%)
  starting transfers between devices  19.7 us (29%)
  local copies, waits for them, and re-layouts  1.92 us (3%)
  other arithmetic  0.86 us (1%)
    ppermute x18, waiting for transfers between devices, flip(): return lax.ppermute(array, axis, [(i, i ^ step) for i in range(size)])  25.1 us
    ppermute x18, starting transfers between devices, flip(): return lax.ppermute(array, axis, [(i, i ^ step) for i in range(size)])  19.7 us
    pallas_call x2, Pallas kernels, chunk_gradient(): pl.pallas_call(lambda *refs: chunk_kernel(groups, 2 * slots, *refs), in_s...  11.9 us
    pallas_call x1, Pallas kernels, load_weights(): pl.pallas_call(load_kernel, in_specs=[HBM] * 3 + [VMEM, SMEM], out_specs=...  8.43 us
  transfers between devices with their start and end apart: 18, of which 10 were waited for; matrix products, arithmetic and copies ran while one was open for 2% of the time, Pallas kernels for 30%

commit v1 on v0

--- a/solution.py
+++ b/solution.py
@@ -180,26 +180,29 @@
             total[...] = term
         else:
             total[...] += term
-    for number in range(count):
-        rows = slice(number * height, (number + 1) * height)
-        out = mine_out if number < count // 2 else other_out
-        for step in range(groups):
-            start = pl.multiple_of((place ^ step) * cols, LANES)
-            part = total[rows, pl.ds(start, cols)]
-            out[number % (count // 2), :, step * cols : (step + 1) * cols] = part.astype(out.dtype)
+    slots = count // 2
+    for out, core in ((mine_out, scalars[2]), (other_out, 1 - scalars[2])):
+        for index in range(groups // 2):
+            start = pl.multiple_of((place ^ (core * (groups - 1)) ^ index) * cols, LANES)
+            for slot in range(slots):
+                for rep in range(2):
+                    first = ((scalars[2] ^ rep) * slots + slot) * height
+                    part = total[pl.ds(pl.multiple_of(first, height), height), pl.ds(start, cols)]
+                    out[slot, index, rep * height : (rep + 1) * height, :] = part.astype(out.dtype)
 
 
 def chunk_gradient(scalars, mine, other, weights, groups):
     local, width, double = weights[0].shape
     slots, height = len(mine), mine[0].shape[0]
     rows = 2 * slots * height
+    shape = (slots, groups // 2, 2 * height, width // groups)
     return pl.pallas_call(
         lambda *refs: chunk_kernel(groups, 2 * slots, *refs),
         in_specs=[SMEM] + [VMEM] * (2 * slots + 3),
         out_specs=[VMEM, VMEM],
         out_shape=[
-            jax.ShapeDtypeStruct((slots, height, width), jnp.float32),
-            jax.ShapeDtypeStruct((slots, height, width), jnp.bfloat16),
+            jax.ShapeDtypeStruct(shape, jnp.float32),
+            jax.ShapeDtypeStruct(shape, jnp.bfloat16),
         ],
         scratch_shapes=[
             pltpu.VMEM((rows, width), jnp.bfloat16),
@@ -216,26 +219,49 @@
     )(scalars, *mine, *other, *weights)
 
 
-def join_kernel(mine, swapped, *outs):
-    for number, out in enumerate(outs):
-        out[...] = (mine[number] + swapped[number].astype(jnp.float32)).astype(out.dtype)
+def join_kernel(kinds, mine, swapped, *outs):
+    for slot, (_, cut) in enumerate(kinds):
+        part = mine[slot] + swapped[slot].astype(jnp.float32)
+        for index in range(part.shape[0] if cut else 1):
+            out, outs = outs[0], outs[1:]
+            out[...] = (part[index] if cut else part).astype(out.dtype)
 
 
 def join(mine, swapped, kinds):
     shape = mine.shape[1:]
-    return pl.pallas_call(
-        join_kernel,
+    shapes = []
+    for kind, cut in kinds:
+        shapes += [jax.ShapeDtypeStruct(shape[1:], kind)] * shape[0] if cut else [jax.ShapeDtypeStruct(shape, kind)]
+    outs = pl.pallas_call(
+        lambda *refs: join_kernel(kinds, *refs),
         in_specs=[VMEM] * 2,
-        out_specs=[VMEM] * len(kinds),
-        out_shape=[jax.ShapeDtypeStruct(shape, kind) for kind in kinds],
+        out_specs=[VMEM] * len(shapes),
+        out_shape=shapes,
         compiler_params=pltpu.CompilerParams(vmem_limit_bytes=1 << 20),
         name="join",
     )(mine, swapped)
+    slots = []
+    for _, cut in kinds:
+        number = shape[0] if cut else 1
+        slots.append(outs[:number])
+        outs = outs[number:]
+    return slots
 
 
 def flip(array, axis, step):
     size = lax.axis_size(axis)
     return lax.ppermute(array, axis, [(i, i ^ step) for i in range(size)])
+
+
+def straight(array, wide_step, index):
+    wide_size, groups = lax.axis_size("wide"), lax.axis_size("grp")
+    pairs = []
+    for w in range(wide_size):
+        for g in range(groups):
+            for r in range(2):
+                target = (w ^ wide_step) * groups + (g ^ (r * (groups - 1)) ^ index)
+                pairs.append(((w * groups + g) * 2 + r, target * 2 + r))
+    return lax.ppermute(array, ("wide", "grp", "rep"), pairs)
 
 
 def route_table(route_ids, route_weights, experts):
@@ -255,14 +281,15 @@
 
 
 def dense_shards(hidden_in, grad_out, route_ids, route_weights, gate_proj, up_proj, down_proj):
-    tok_rows, cols = hidden_in.shape
+    tok_rows, _ = hidden_in.shape
     wide_size = lax.axis_size("wide")
     groups = lax.axis_size("grp")
     local = gate_proj.shape[0]
     height = tok_rows // groups
     place = lax.axis_index("grp").astype(jnp.int32)
     wide = lax.axis_index("wide").astype(jnp.int32)
-    scalars = jnp.stack([place, wide])
+    rep = lax.axis_index("rep").astype(jnp.int32)
+    scalars = jnp.stack([place, wide, rep])
 
     pieces = []
     for step in range(groups):
@@ -281,25 +308,41 @@
     weights = load_weights(gate_proj, up_proj, down_proj, block, scalars)
     blocks = gathered(block, "wide")
     half_way = wide_size // 2
+    last = wide_size - 1
     order = [k for k in range(1, wide_size)] + [0]
-    chunks = [order[i : i + half_way] for i in range(0, wide_size, half_way)] if half_way else [[0]]
-    others = [flip(b, "rep", 1) for b in blocks]
-    summed = jnp.zeros((height, cols * groups), jnp.float32)
+    chunks = [order[i : i + half_way] for i in range(0, wide_size, half_way)]
+    others = []
+    for k in range(wide_size):
+        others.append(flip(blocks[k], "rep", 1))
+    near = None
     for chunk in chunks:
         mine, other = chunk_gradient(
             scalars, [blocks[k] for k in chunk], [others[k] for k in chunk], weights, groups
         )
-        kinds = [jnp.bfloat16 if k else jnp.float32 for k in chunk]
-        for k, part in zip(chunk, join(mine, flip(other, "rep", 1), kinds)):
+        swapped = flip(other, "rep", 1)
+        kinds = [(jnp.bfloat16 if k else jnp.float32, k == last) for k in chunk]
+        for k, parts in zip(chunk, join(mine, swapped, kinds)):
+            if k == last:
+                far = []
+                for index, part in enumerate(parts):
+                    far.append(straight(part, k, index))
+                continue
+            part = parts[0]
             if k:
                 part = flip(part, "wide", k)
-                part = part.astype(jnp.float32)
-            summed = summed + part
-    summed = summed.astype(jnp.bfloat16)
-    pieces = []
-    for step in range(groups):
-        piece = summed[:, step * cols : (step + 1) * cols]
-        pieces.append(piece if step == 0 else flip(piece, "grp", step))
+            part = part.astype(jnp.float32)
+            near = part if near is None else part + near
+    first_core = rep == 0
+    keep, give = [], []
+    for index in range(groups // 2):
+        piece = straight(near[index].astype(jnp.bfloat16), 0, index)
+        piece = piece.astype(jnp.float32) + far[index].astype(jnp.float32)
+        piece = piece.astype(jnp.bfloat16)
+        keep.append(jnp.where(first_core, piece[:height], piece[height:]))
+        give.append(jnp.where(first_core, piece[height:], piece[:height]))
+    taken = flip(jnp.concatenate(give[::-1], axis=0), "rep", 1)
+    pieces = keep + [taken[i * height : (i + 1) * height] for i in range(groups // 2)]
+    place = place ^ (rep * (groups - 1))
     bit = 1
     while bit < groups:
         swap = (place & bit) != 0
@@ -312,7 +355,7 @@
     wide_size, groups = lax.axis_size("wide"), lax.axis_size("grp")
     experts = gate_proj.shape[0] * wide_size
     fanout = route_ids.shape[1]
-    powers = all(n & (n - 1) == 0 for n in (wide_size, groups))
+    powers = all(n > 1 and n & (n - 1) == 0 for n in (wide_size, groups))
     dense = powers and experts <= 2 * fanout and 2 * experts <= LANES and lax.axis_size("rep") == 2
     path = dense_shards if dense else routed_shards
     return path(

time: 68.5 us -> 70.5 us (1.029)
  starting transfers between devices: 19.7 us -> 22.3 us
    ppermute x0 -> x4, starting transfers between devices: none -> 6.07 us  [straight(): return lax.ppermute(array, ('wide', 'grp', 'rep'), pairs)]
    ppermute x18 -> x15, waiting for transfers between devices: 25.1 us -> 21.3 us  [flip(): return lax.ppermute(array, axis, [(i, i ^ step) for i in range(size)])]
    ppermute x18 -> x15, starting transfers between devices: 19.7 us -> 16.2 us  [flip(): return lax.ppermute(array, axis, [(i, i ^ step) for i in range(size)])]
    ppermute x0 -> x4, waiting for transfers between devices: none -> 3.26 us  [straight(): return lax.ppermute(array, ('wide', 'grp', 'rep'), pairs)]
  transfers between devices with their start and end apart: 18 -> 19, of which waited for: 10 -> 9; matrix products, arithmetic and copies ran while one was open for 2% -> 1% of each run, Pallas kernels for 30% -> 29%
where the time goes in v1:
time: 70.5 us; the launch traced here: 70.3 us
  waiting for transfers between devices  24.6 us (35%)
  starting transfers between devices  22.3 us (32%)
  Pallas kernels  20.4 us (29%)
  local copies, waits for them, and re-layouts  1.92 us (3%)
  other arithmetic  0.92 us (1%)
    ppermute x15, waiting for transfers between devices, flip(): return lax.ppermute(array, axis, [(i, i ^ step) for i in range(size)])  21.3 us
    ppermute x15, starting transfers between devices, flip(): return lax.ppermute(array, axis, [(i, i ^ step) for i in range(size)])  16.2 us
    pallas_call x2, Pallas kernels, chunk_gradient(): pl.pallas_call(lambda *refs: chunk_kernel(groups, 2 * slots, *refs), in_s...  11.9 us
    pallas_call x1, Pallas kernels, load_weights(): pl.pallas_call(load_kernel, in_specs=[HBM] * 3 + [VMEM, SMEM], out_specs=...  8.43 us
    ppermute x4, starting transfers between devices, straight(): return lax.ppermute(array, ('wide', 'grp', 'rep'), pairs)  6.07 us
    ppermute x4, waiting for transfers between devices, straight(): return lax.ppermute(array, ('wide', 'grp', 'rep'), pairs)  3.26 us
  transfers between devices with their start and end apart: 19, of which 9 were waited for; matrix products, arithmetic and copies ran while one was open for 1% of the time, Pallas kernels for 29%

profile of v1, /device:TPU:0, one launch (start us, length us, event | category | flops | bytes accessed | tf_op | source)
XLA Modules:
  0.0 70.3 jit_solution(17402799880919061513)
XLA Ops:
  0.0 0.0 copy-start
  0.0 0.9 %constant_dynamic-slice_fusion.2 = (bf16[32,512]{1,0:T(8,128)(2,1)S(1)}, bf16[32,512]{1,0:T(8,128)(2,1)S(1)}, bf16[32,512]{1,0:T(8,128)(2,1)S(1)}, bf16[32,512]{...) fusion(bf16[128,512]{1,0:T(8,128)(2,1)} %param.8, ...), kind=kLoop, calls=%fused_computation.28 | loop fusion | bytes 524304 | tf_op jit(solution)/shard_map/dynamic_slice | solution.py:298
  0.9 4.0 %collective-permute-start.2 = (bf16[32,1024]{1,0:T(8,128)(2,1)S(1)}, bf16[32,1024]{1,0:T(8,128)(2,1)S(1)}, u32[]{:S(2)}, u32[]{:S(2)}) collective-permute-start(bf16[32,1024]{1,0:T(8,128)(2,1)S(1)} %pad_maximum_fusion.3), channel_id=1, source_target_pairs={{0,6},{2,4},{4,2},{6,0},{1,7},{3,5},{5,3},{7,1},{8,14},{10,12},{12... | collective-permute-start | bytes 196616 | tf_op jit(solution)/shard_map/ppermute | solution.py:253
  4.9 0.5 collective-permute-start.1
  5.4 0.1 collective-permute-start
  5.6 0.0 copy-done
  5.6 0.1 constant_dynamic-slice_fusion
  5.6 0.8 %constant_dynamic-slice_fusion.1 = s32[32,8]{0,1:T(8,128)S(1)} fusion(s32[128,8]{0,1:T(8,128)} %param.9, s32[]{:T(128)S(6)} %select_n.81), kind=kLoop, calls=%fused_computation.27 | loop fusion | bytes 2052 | tf_op jit(solution)/shard_map/dynamic_slice | solution.py:301
  6.4 0.1 copy.10
  6.5 0.6 collective-permute-done.2
  7.2 2.0 %collective-permute-done.1 = bf16[32,1024]{1,0:T(8,128)(2,1)S(1)} collective-permute-done((bf16[32,1024]{1,0:T(8,128)(2,1)S(1)}, bf16[32,1024]{1,0:T(8,128)(2,1)S(1)}, u32[]{:S(2)}, u32[]{:S(2)}) %collective-permute-start.1) | collective-permute-done | bytes 65568 | tf_op jit(solution)/shard_map/ppermute | solution.py:253
  9.2 0.5 collective-permute-done
  9.7 0.1 concatenate.21.after.refs_2_
  9.8 2.6 %collective-permute-start.3 = (bf16[32,4224]{1,0:T(8,128)(2,1)S(1)}, bf16[32,4224]{1,0:T(8,128)(2,1)S(1)}, u32[]{:S(2)}, u32[]{:S(2)}) collective-permute-start(bf16[32,4224]{1,0:T(8,128)(2,1)S(1)} %concatenate.21.after.refs_2_), channel_id=1, source_target_pairs={{0,16},{8,24},{16,0},{24,8},{1,17},{9,25},{17,1},{25,9},{2,18},{10... | collective-permute-start | bytes 811016 | tf_op jit(solution)/shard_map/ppermute | solution.py:253
  12.4 1.6 %collective-permute-start.8 = (bf16[32,4224]{1,0:T(8,128)(2,1)S(1)}, bf16[32,4224]{1,0:T(8,128)(2,1)S(1)}, u32[]{:S(2)}, u32[]{:S(2)}) collective-permute-start(bf16[32,4224]{1,0:T(8,128)(2,1)S(1)} %concatenate.21.after.refs_2_), channel_id=1, source_target_pairs={{0,8},{8,0},{16,24},{24,16},{1,9},{9,1},{17,25},{25,17},{2,10},{10... | collective-permute-start | bytes 811016 | tf_op jit(solution)/shard_map/ppermute | solution.py:253
  14.0 9.5 %collective-permute-done.3.refs_2_ = bf16[32,4224]{1,0:T(8,128)(2,1)S(1)} collective-permute-done((bf16[32,4224]{1,0:T(8,128)(2,1)S(1)}, bf16[32,4224]{1,0:T(8,128)(2,1)S(1)}, u32[]{:S(2)}, u32[]{:S(2)}) %collective-permute-start.3) | collective-permute-done | bytes 270368 | tf_op jit(solution)/shard_map/ppermute | solution.py:253
  23.5 0.6 collective-permute-start.4
  24.1 0.0 collective-permute-start.10
  24.1 0.0 collective-permute-done.8.refs_1_
  24.1 0.5 collective-permute-start.9
  24.6 0.1 pad_add_fusion.scalars.refs_0_
  24.7 0.0 collective-permute-start.6
  24.7 8.4 %load.1 = (bf16[4,2048,768]{2,1,0:T(8,128)(2,1)S(1)}, bf16[4,768,2048]{2,1,0:T(8,128)(2,1)S(1)}, bf16[2048,1536]{1,0:T(8,128)(2,1)S(1)}) custom-call(bf16[4,2048,384]{2,1,0:T(8,128)(2,1)} %gate_hbm.1, bf16[4,2048,384]{2,1,0:T(8,128)(2,1)} %up_hbm.1, bf16[4,384,2048]{2,1,0:T(8,128)(2,1)} %down_hbm.1, bf16[32,4224]{1,0:T(8,128)(2,1)S(1)} %concatenate.21.after.refs_2_, ...), custom_call_target="tpu_custom_call" | custom-call | bytes 18874368 | tf_op jit(solution)/shard_map/load/pallas_call | solution.py:123
  33.2 0.0 collective-permute-done.4.refs_1_
  33.2 0.6 collective-permute-start.5
  33.7 0.0 collective-permute-done.10.refs_4_
  33.7 0.0 collective-permute-done.9.refs_3_
  33.7 5.8 %chunk.3 = (f32[2,2,64,512]{3,2,1,0:T(8,128)S(1)}, bf16[2,2,64,512]{3,2,1,0:T(8,128)(2,1)S(1)}) custom-call(s32[3]{0:T(128)S(1)} %pad_add_fusion.scalars.refs_0_, bf16[32,4224]{1,0:T(8,128)(2,1)S(1)} %collective-permute-done.8.refs_1_, bf16[32,4224]{1,0:T(8,128)(2,1)S(1)} %collective-permute-done.3.refs_2_, ...), custom_call_target="tpu_custom_call" | custom-call | flops 4026531840 | bytes 1048576 | tf_op jit(solution)/shard_map/chunk/pallas_call | solution.py:199
  39.6 0.1 collective-permute-start.11
  39.7 0.0 collective-permute-done.6.refs_4_
  39.7 0.0 collective-permute-done.5.refs_3_
  39.7 6.0 %chunk.2 = (f32[2,2,64,512]{3,2,1,0:T(8,128)S(1)}, bf16[2,2,64,512]{3,2,1,0:T(8,128)(2,1)S(1)}) custom-call(s32[3]{0:T(128)S(1)} %pad_add_fusion.scalars.refs_0_, bf16[32,4224]{1,0:T(8,128)(2,1)S(1)} %collective-permute-done.4.refs_1_, bf16[32,4224]{1,0:T(8,128)(2,1)S(1)} %concatenate.21.after.refs_2_, bf16[32,4224]{1,0:T(8,128)(2,1)S(1)} %collective-permute-done.5.refs_3_, ...), custom_call_target="tpu_custom_call" | custom-call | flops 4026531840 | bytes 1048576 | tf_op jit(solution)/shard_map/chunk/pallas_call | solution.py:199
  45.7 0.5 collective-permute-start.7
  46.3 0.0 collective-permute-done.11.refs_1_
  46.3 0.1 join.3
  46.3 3.4 %collective-permute-start.12 = (bf16[2,64,512]{2,1,0:T(8,128)(2,1)S(1)}, bf16[2,64,512]{2,1,0:T(8,128)(2,1)S(1)}, u32[]{:S(2)}, u32[]{:S(2)}) collective-permute-start(bf16[2,64,512]{2,1,0:T(8,128)(2,1)S(1)} %get-tuple-element.25), channel_id=1, source_target_pairs={{0,16},{8,24},{16,0},{24,8},{1,17},{9,25},{17,1},{25,9},{2,18},{10... | collective-permute-start | bytes 393224 | tf_op jit(solution)/shard_map/ppermute | solution.py:253
  49.8 0.0 collective-permute-start.13
  49.8 0.0 collective-permute-done.7.refs_1_
  49.8 6.6 %collective-permute-done.12 = bf16[2,64,512]{2,1,0:T(8,128)(2,1)S(1)} collective-permute-done((bf16[2,64,512]{2,1,0:T(8,128)(2,1)S(1)}, bf16[2,64,512]{2,1,0:T(8,128)(2,1)S(1)}, u32[]{:S(2)}, u32[]{:S(2)}) %collective-permute-start.12) | collective-permute-done | bytes 131104 | tf_op jit(solution)/shard_map/ppermute | solution.py:253
  56.4 1.1 %collective-permute-done.13 = bf16[2,64,512]{2,1,0:T(8,128)(2,1)S(1)} collective-permute-done((bf16[2,64,512]{2,1,0:T(8,128)(2,1)S(1)}, bf16[2,64,512]{2,1,0:T(8,128)(2,1)S(1)}, u32[]{:S(2)}, u32[]{:S(2)}) %collective-permute-start.13) | collective-permute-done | bytes 131104 | tf_op jit(solution)/shard_map/ppermute | solution.py:253
  57.6 1.5 %collective-permute-start.14 = (bf16[64,512]{1,0:T(8,128)(2,1)S(1)}, bf16[64,512]{1,0:T(8,128)(2,1)S(1)}, u32[]{:S(2)}, u32[]{:S(2)}) collective-permute-start(bf16[64,512]{1,0:T(8,128)(2,1)S(1)} %get-tuple-element.35), channel_id=1, source_target_pairs={{0,2},{1,5},{2,0},{3,7},{4,6},{5,1},{6,4},{7,3},{8,10},{9,13},{10,... | collective-permute-start | bytes 196616 | tf_op jit(solution)/shard_map/ppermute | solution.py:264
  59.1 1.0 %collective-permute-start.15 = (bf16[64,512]{1,0:T(8,128)(2,1)S(1)}, bf16[64,512]{1,0:T(8,128)(2,1)S(1)}, u32[]{:S(2)}, u32[]{:S(2)}) collective-permute-start(bf16[64,512]{1,0:T(8,128)(2,1)S(1)} %get-tuple-element.27), channel_id=1, source_target_pairs={{0,26},{1,29},{2,24},{3,31},{4,30},{5,25},{6,28},{7,27},{8,18},{9,... | collective-permute-start | bytes 196616 | tf_op jit(solution)/shard_map/ppermute | solution.py:264
  60.0 0.7 collective-permute-start.16
  60.7 2.9 %collective-permute-start.17 = (bf16[64,512]{1,0:T(8,128)(2,1)S(1)}, bf16[64,512]{1,0:T(8,128)(2,1)S(1)}, u32[]{:S(2)}, u32[]{:S(2)}) collective-permute-start(bf16[64,512]{1,0:T(8,128)(2,1)S(1)} %get-tuple-element.28), channel_id=1, source_target_pairs={{0,24},{1,31},{2,26},{3,29},{4,28},{5,27},{6,30},{7,25},{8,16},{9,... | collective-permute-start | bytes 196616 | tf_op jit(solution)/shard_map/ppermute | solution.py:264
  63.7 0.0 collective-permute-done.14
  63.7 2.5 %collective-permute-done.15 = bf16[64,512]{1,0:T(8,128)(2,1)S(1)} collective-permute-done((bf16[64,512]{1,0:T(8,128)(2,1)S(1)}, bf16[64,512]{1,0:T(8,128)(2,1)S(1)}, u32[]{:S(2)}, u32[]{:S(2)}) %collective-permute-start.15) | collective-permute-done | bytes 65568 | tf_op jit(solution)/shard_map/ppermute | solution.py:264
  66.2 0.0 collective-permute-done.16
  66.2 0.8 %collective-permute-done.17 = bf16[64,512]{1,0:T(8,128)(2,1)S(1)} collective-permute-done((bf16[64,512]{1,0:T(8,128)(2,1)S(1)}, bf16[64,512]{1,0:T(8,128)(2,1)S(1)}, u32[]{:S(2)}, u32[]{:S(2)}) %collective-permute-start.17) | collective-permute-done | bytes 65568 | tf_op jit(solution)/shard_map/ppermute | solution.py:264
  67.0 1.6 %collective-permute-start.18 = (bf16[64,512]{1,0:T(8,128)(2,1)S(1)}, bf16[64,512]{1,0:T(8,128)(2,1)S(1)}, u32[]{:S(2)}, u32[]{:S(2)}) collective-permute-start(bf16[64,512]{1,0:T(8,128)(2,1)S(1)} %pad_maximum_fusion.4), channel_id=1, source_target_pairs={{0,1},{1,0},{2,3},{3,2},{4,5},{5,4},{6,7},{7,6},{8,9},{9,8},{10,11... | collective-permute-start | bytes 196616 | tf_op jit(solution)/shard_map/ppermute | solution.py:253
  68.6 0.9 %collective-permute-done.18 = bf16[64,512]{1,0:T(8,128)(2,1)S(1)} collective-permute-done((bf16[64,512]{1,0:T(8,128)(2,1)S(1)}, bf16[64,512]{1,0:T(8,128)(2,1)S(1)}, u32[]{:S(2)}, u32[]{:S(2)}) %collective-permute-start.18) | collective-permute-done | bytes 65568 | tf_op jit(solution)/shard_map/ppermute | solution.py:253
  69.6 0.7 pad_maximum_fusion
  (16 shorter events, 0.2 us)
Async XLA Ops:
  0.0 5.6 %copy-start = (f32[128,8]{0,1:T(8,128)S(1)}, f32[128,8]{0,1:T(8,128)}, u32[]{:S(2)}) copy-start(f32[128,8]{0,1:T(8,128)} %param.10) | copy-start | bytes 12292
  0.9 6.2 %collective-permute-start.2 = (bf16[32,1024]{1,0:T(8,128)(2,1)S(1)}, bf16[32,1024]{1,0:T(8,128)(2,1)S(1)}, u32[]{:S(2)}, u32[]{:S(2)}) collective-permute-start(bf16[32,1024]{1,0:T(8,128)(2,1)S(1)} %pad_maximum_fusion.3), channel_id=1, source_target_pairs={{0,6},{2,4},{4,2},{6,0},{1,7},{3,5},{5,3},{7,1},{8,14},{10,12},{12... | collective-permute-start | bytes 196616 | tf_op jit(solution)/shard_map/ppermute | solution.py:253
  4.9 4.3 %collective-permute-start.1 = (bf16[32,1024]{1,0:T(8,128)(2,1)S(1)}, bf16[32,1024]{1,0:T(8,128)(2,1)S(1)}, u32[]{:S(2)}, u32[]{:S(2)}) collective-permute-start(bf16[32,1024]{1,0:T(8,128)(2,1)S(1)} %pad_maximum_fusion.2), channel_id=1, source_target_pairs={{0,4},{2,6},{4,0},{6,2},{1,5},{3,7},{5,1},{7,3},{8,12},{10,14},{12... | collective-permute-start | bytes 196616 | tf_op jit(solution)/shard_map/ppermute | solution.py:253
  5.4 4.3 %collective-permute-start = (bf16[32,1024]{1,0:T(8,128)(2,1)S(1)}, bf16[32,1024]{1,0:T(8,128)(2,1)S(1)}, u32[]{:S(2)}, u32[]{:S(2)}) collective-permute-start(bf16[32,1024]{1,0:T(8,128)(2,1)S(1)} %pad_maximum_fusion.1), channel_id=1, source_target_pairs={{0,2},{2,0},{4,6},{6,4},{1,3},{3,1},{5,7},{7,5},{8,10},{10,8},{12,... | collective-permute-start | bytes 196616 | tf_op jit(solution)/shard_map/ppermute | solution.py:253
  9.8 13.7 %collective-permute-start.3 = (bf16[32,4224]{1,0:T(8,128)(2,1)S(1)}, bf16[32,4224]{1,0:T(8,128)(2,1)S(1)}, u32[]{:S(2)}, u32[]{:S(2)}) collective-permute-start(bf16[32,4224]{1,0:T(8,128)(2,1)S(1)} %concatenate.21.after.refs_2_), channel_id=1, source_target_pairs={{0,16},{8,24},{16,0},{24,8},{1,17},{9,25},{17,1},{25,9},{2,18},{10... | collective-permute-start | bytes 811016 | tf_op jit(solution)/shard_map/ppermute | solution.py:253
  12.4 11.7 %collective-permute-start.8 = (bf16[32,4224]{1,0:T(8,128)(2,1)S(1)}, bf16[32,4224]{1,0:T(8,128)(2,1)S(1)}, u32[]{:S(2)}, u32[]{:S(2)}) collective-permute-start(bf16[32,4224]{1,0:T(8,128)(2,1)S(1)} %concatenate.21.after.refs_2_), channel_id=1, source_target_pairs={{0,8},{8,0},{16,24},{24,16},{1,9},{9,1},{17,25},{25,17},{2,10},{10... | collective-permute-start | bytes 811016 | tf_op jit(solution)/shard_map/ppermute | solution.py:253
  23.5 9.6 %collective-permute-start.4 = (bf16[32,4224]{1,0:T(8,128)(2,1)S(1)}, bf16[32,4224]{1,0:T(8,128)(2,1)S(1)}, u32[]{:S(2)}, u32[]{:S(2)}) collective-permute-start(bf16[32,4224]{1,0:T(8,128)(2,1)S(1)} %collective-permute-done.3.refs_2_), channel_id=1, source_target_pairs={{0,8},{8,0},{16,24},{24,16},{1,9},{9,1},{17,25},{25,17},{2,10},{10... | collective-permute-start | bytes 811016 | tf_op jit(solution)/shard_map/ppermute | solution.py:253
  24.1 9.6 %collective-permute-start.10 = (bf16[32,4224]{1,0:T(8,128)(2,1)S(1)}, bf16[32,4224]{1,0:T(8,128)(2,1)S(1)}, u32[]{:S(2)}, u32[]{:S(2)}) collective-permute-start(bf16[32,4224]{1,0:T(8,128)(2,1)S(1)} %collective-permute-done.3.refs_2_), channel_id=1, source_target_pairs={{0,1},{1,0},{2,3},{3,2},{4,5},{5,4},{6,7},{7,6},{8,9},{9,8},{10,11... | collective-permute-start | bytes 811016 | tf_op jit(solution)/shard_map/ppermute | solution.py:253
  24.1 9.6 %collective-permute-start.9 = (bf16[32,4224]{1,0:T(8,128)(2,1)S(1)}, bf16[32,4224]{1,0:T(8,128)(2,1)S(1)}, u32[]{:S(2)}, u32[]{:S(2)}) collective-permute-start(bf16[32,4224]{1,0:T(8,128)(2,1)S(1)} %collective-permute-done.8.refs_1_), channel_id=1, source_target_pairs={{0,1},{1,0},{2,3},{3,2},{4,5},{5,4},{6,7},{7,6},{8,9},{9,8},{10,11... | collective-permute-start | bytes 811016 | tf_op jit(solution)/shard_map/ppermute | solution.py:253
  24.7 15.0 %collective-permute-start.6 = (bf16[32,4224]{1,0:T(8,128)(2,1)S(1)}, bf16[32,4224]{1,0:T(8,128)(2,1)S(1)}, u32[]{:S(2)}, u32[]{:S(2)}) collective-permute-start(bf16[32,4224]{1,0:T(8,128)(2,1)S(1)} %concatenate.21.after.refs_2_), channel_id=1, source_target_pairs={{0,1},{1,0},{2,3},{3,2},{4,5},{5,4},{6,7},{7,6},{8,9},{9,8},{10,11... | collective-permute-start | bytes 811016 | tf_op jit(solution)/shard_map/ppermute | solution.py:253
  33.2 6.5 %collective-permute-start.5 = (bf16[32,4224]{1,0:T(8,128)(2,1)S(1)}, bf16[32,4224]{1,0:T(8,128)(2,1)S(1)}, u32[]{:S(2)}, u32[]{:S(2)}) collective-permute-start(bf16[32,4224]{1,0:T(8,128)(2,1)S(1)} %collective-permute-done.4.refs_1_), channel_id=1, source_target_pairs={{0,1},{1,0},{2,3},{3,2},{4,5},{5,4},{6,7},{7,6},{8,9},{9,8},{10,11... | collective-permute-start | bytes 811016 | tf_op jit(solution)/shard_map/ppermute | solution.py:253
  39.6 6.7 %collective-permute-start.11 = (bf16[2,2,64,512]{3,2,1,0:T(8,128)(2,1)S(1)}, bf16[2,2,64,512]{3,2,1,0:T(8,128)(2,1)S(1)}, u32[]{:S(2)}, u32[]{:S(2)}) collective-permute-start(bf16[2,2,64,512]{3,2,1,0:T(8,128)(2,1)S(1)} %get-tuple-element.24), channel_id=1, source_target_pairs={{0,1},{1,0},{2,3},{3,2},{4,5},{5,4},{6,7},{7,6},{8,9},{9,8},{10,11... | collective-permute-start | bytes 786440 | tf_op jit(solution)/shard_map/ppermute | solution.py:253
  45.7 4.0 %collective-permute-start.7 = (bf16[2,2,64,512]{3,2,1,0:T(8,128)(2,1)S(1)}, bf16[2,2,64,512]{3,2,1,0:T(8,128)(2,1)S(1)}, u32[]{:S(2)}, u32[]{:S(2)}) collective-permute-start(bf16[2,2,64,512]{3,2,1,0:T(8,128)(2,1)S(1)} %get-tuple-element.21), channel_id=1, source_target_pairs={{0,1},{1,0},{2,3},{3,2},{4,5},{5,4},{6,7},{7,6},{8,9},{9,8},{10,11... | collective-permute-start | bytes 786440 | tf_op jit(solution)/shard_map/ppermute | solution.py:253
  46.3 10.0 %collective-permute-start.12 = (bf16[2,64,512]{2,1,0:T(8,128)(2,1)S(1)}, bf16[2,64,512]{2,1,0:T(8,128)(2,1)S(1)}, u32[]{:S(2)}, u32[]{:S(2)}) collective-permute-start(bf16[2,64,512]{2,1,0:T(8,128)(2,1)S(1)} %get-tuple-element.25), channel_id=1, source_target_pairs={{0,16},{8,24},{16,0},{24,8},{1,17},{9,25},{17,1},{25,9},{2,18},{10... | collective-permute-start | bytes 393224 | tf_op jit(solution)/shard_map/ppermute | solution.py:253
  49.8 7.7 %collective-permute-start.13 = (bf16[2,64,512]{2,1,0:T(8,128)(2,1)S(1)}, bf16[2,64,512]{2,1,0:T(8,128)(2,1)S(1)}, u32[]{:S(2)}, u32[]{:S(2)}) collective-permute-start(bf16[2,64,512]{2,1,0:T(8,128)(2,1)S(1)} %get-tuple-element.26), channel_id=1, source_target_pairs={{0,8},{8,0},{16,24},{24,16},{1,9},{9,1},{17,25},{25,17},{2,10},{10... | collective-permute-start | bytes 393224 | tf_op jit(solution)/shard_map/ppermute | solution.py:253
  57.6 6.1 %collective-permute-start.14 = (bf16[64,512]{1,0:T(8,128)(2,1)S(1)}, bf16[64,512]{1,0:T(8,128)(2,1)S(1)}, u32[]{:S(2)}, u32[]{:S(2)}) collective-permute-start(bf16[64,512]{1,0:T(8,128)(2,1)S(1)} %get-tuple-element.35), channel_id=1, source_target_pairs={{0,2},{1,5},{2,0},{3,7},{4,6},{5,1},{6,4},{7,3},{8,10},{9,13},{10,... | collective-permute-start | bytes 196616 | tf_op jit(solution)/shard_map/ppermute | solution.py:264
  59.1 7.1 %collective-permute-start.15 = (bf16[64,512]{1,0:T(8,128)(2,1)S(1)}, bf16[64,512]{1,0:T(8,128)(2,1)S(1)}, u32[]{:S(2)}, u32[]{:S(2)}) collective-permute-start(bf16[64,512]{1,0:T(8,128)(2,1)S(1)} %get-tuple-element.27), channel_id=1, source_target_pairs={{0,26},{1,29},{2,24},{3,31},{4,30},{5,25},{6,28},{7,27},{8,18},{9,... | collective-permute-start | bytes 196616 | tf_op jit(solution)/shard_map/ppermute | solution.py:264
  60.0 6.1 %collective-permute-start.16 = (bf16[64,512]{1,0:T(8,128)(2,1)S(1)}, bf16[64,512]{1,0:T(8,128)(2,1)S(1)}, u32[]{:S(2)}, u32[]{:S(2)}) collective-permute-start(bf16[64,512]{1,0:T(8,128)(2,1)S(1)} %get-tuple-element.36), channel_id=1, source_target_pairs={{0,0},{1,7},{2,2},{3,5},{4,4},{5,3},{6,6},{7,1},{8,8},{9,15},{10,1... | collective-permute-start | bytes 196616 | tf_op jit(solution)/shard_map/ppermute | solution.py:264
  60.7 6.3 %collective-permute-start.17 = (bf16[64,512]{1,0:T(8,128)(2,1)S(1)}, bf16[64,512]{1,0:T(8,128)(2,1)S(1)}, u32[]{:S(2)}, u32[]{:S(2)}) collective-permute-start(bf16[64,512]{1,0:T(8,128)(2,1)S(1)} %get-tuple-element.28), channel_id=1, source_target_pairs={{0,24},{1,31},{2,26},{3,29},{4,28},{5,27},{6,30},{7,25},{8,16},{9,... | collective-permute-start | bytes 196616 | tf_op jit(solution)/shard_map/ppermute | solution.py:264
  67.0 2.5 %collective-permute-start.18 = (bf16[64,512]{1,0:T(8,128)(2,1)S(1)}, bf16[64,512]{1,0:T(8,128)(2,1)S(1)}, u32[]{:S(2)}, u32[]{:S(2)}) collective-permute-start(bf16[64,512]{1,0:T(8,128)(2,1)S(1)} %pad_maximum_fusion.4), channel_id=1, source_target_pairs={{0,1},{1,0},{2,3},{3,2},{4,5},{5,4},{6,7},{7,6},{8,9},{9,8},{10,11... | collective-permute-start | bytes 196616 | tf_op jit(solution)/shard_map/ppermute | solution.py:253

commit v2 on v1

--- a/solution.py
+++ b/solution.py
@@ -96,24 +96,24 @@
 HBM = pl.BlockSpec(memory_space=pltpu.HBM)
 
 
-def load_kernel(gate_hbm, up_hbm, down_hbm, after, scalars, both, both_t, down_t, down, sems):
+def load_kernel(gate_hbm, up_hbm, down_hbm, after, scalars, both, both_t, down, sems):
     local, _, half = gate_hbm.shape
-    copies = []
+    halves = (pl.ds(0, half), pl.ds(half, half))
+    copies, down_copies = [], []
     for e in range(local):
-        copies.append(
-            (
-                pltpu.make_async_copy(gate_hbm.at[e], both.at[e, :, :half], sems.at[e, 0]),
-                pltpu.make_async_copy(up_hbm.at[e], both.at[e, :, half:], sems.at[e, 1]),
-                pltpu.make_async_copy(down_hbm.at[e], down.at[e], sems.at[e, 2]),
-            )
-        )
-        for copy in copies[e]:
-            copy.start()
-    for e in range(local):
-        for copy in copies[e]:
-            copy.wait()
-        both_t[e] = both[e].T
-        down_t[:, e * half : (e + 1) * half] = down[e].T
+        for number, source in enumerate((gate_hbm, up_hbm)):
+            place = both.at[e, :, halves[number]]
+            copies.append(pltpu.make_async_copy(source.at[e], place, sems.at[e, number]))
+        place = down.at[pl.ds(e * half, half), :]
+        down_copies.append(pltpu.make_async_copy(down_hbm.at[e], place, sems.at[e, 2]))
+    for copy in copies + down_copies:
+        copy.start()
+    for number, copy in enumerate(copies):
+        copy.wait()
+        e, side = divmod(number, 2)
+        both_t[e, side * half : (side + 1) * half] = both[e, :, side * half : (side + 1) * half].T
+    for copy in down_copies:
+        copy.wait()
 
 
 def load_weights(gate_proj, up_proj, down_proj, after, scalars):
@@ -127,22 +127,22 @@
         out_shape=[
             jax.ShapeDtypeStruct((local, width, 2 * half), jnp.bfloat16),
             jax.ShapeDtypeStruct((local, 2 * half, width), jnp.bfloat16),
-            jax.ShapeDtypeStruct((width, local * half), jnp.bfloat16),
+            jax.ShapeDtypeStruct((local * half, width), jnp.bfloat16),
         ],
-        scratch_shapes=[
-            pltpu.VMEM(down_proj.shape, jnp.bfloat16),
-            pltpu.SemaphoreType.DMA((local, 3)),
-        ],
+        scratch_shapes=[pltpu.SemaphoreType.DMA((local, 3))],
         compiler_params=pltpu.CompilerParams(vmem_limit_bytes=8 << 20),
         cost_estimate=pl.CostEstimate(flops=0, bytes_accessed=size, transcendentals=0),
         name="load",
     )(*weights, after, scalars)
 
 
-def chunk_kernel(groups, count, scalars, *refs):
+def chunk_kernel(groups, count, turn, scalars, *refs):
     place, wide = scalars[0], scalars[1]
     blocks = refs[:count]
-    both, both_t, down_t, mine_out, other_out, x_rows, g_rows, total = refs[count:]
+    if turn:
+        both, both_t, down, mine_out, other_out, down_t, x_rows, g_rows, total = refs[count:]
+    else:
+        both, both_t, down_t, mine_out, other_out, x_rows, g_rows, total = refs[count:]
     local, width, double = both.shape
     half = double // 2
     height = blocks[0].shape[0]
@@ -161,14 +161,16 @@
     for e in range(local):
         named = (lane == wide * local + e) | (lane == wide * local + e + experts)
         route = jnp.sum(jnp.where(named, weights, 0.0), axis=1, keepdims=True)
-        pre = jnp.dot(x_rows[...], both[e], preferred_element_type=jnp.float32)
         if e % 2 == 0:
-            paired = min(2, local - e)
+            pair = slice(e * half, (e + min(2, local - e)) * half)
+            if turn:
+                down_t[:, pair] = down[pair].T
             back_pair = jnp.dot(
                 g_rows[...],
-                down_t[:, e * half : (e + paired) * half],
+                down_t[:, pair],
                 preferred_element_type=jnp.float32,
             )
+        pre = jnp.dot(x_rows[...], both[e], preferred_element_type=jnp.float32)
         back = route * back_pair[:, (e % 2) * half : (e % 2 + 1) * half]
         pre_gate, pre_up = pre[:, :half], pre[:, half:]
         sig = 1.0 / (1.0 + jnp.exp(-pre_gate))
@@ -191,19 +193,20 @@
                     out[slot, index, rep * height : (rep + 1) * height, :] = part.astype(out.dtype)
 
 
-def chunk_gradient(scalars, mine, other, weights, groups):
+def chunk_gradient(scalars, mine, other, weights, groups, turn):
     local, width, double = weights[0].shape
     slots, height = len(mine), mine[0].shape[0]
     rows = 2 * slots * height
     shape = (slots, groups // 2, 2 * height, width // groups)
     return pl.pallas_call(
-        lambda *refs: chunk_kernel(groups, 2 * slots, *refs),
+        lambda *refs: chunk_kernel(groups, 2 * slots, turn, *refs),
         in_specs=[SMEM] + [VMEM] * (2 * slots + 3),
-        out_specs=[VMEM, VMEM],
+        out_specs=[VMEM] * (3 if turn else 2),
         out_shape=[
             jax.ShapeDtypeStruct(shape, jnp.float32),
             jax.ShapeDtypeStruct(shape, jnp.bfloat16),
-        ],
+        ]
+        + [jax.ShapeDtypeStruct(weights[2].shape[::-1], jnp.bfloat16)] * turn,
         scratch_shapes=[
             pltpu.VMEM((rows, width), jnp.bfloat16),
             pltpu.VMEM((rows, width), jnp.bfloat16),
@@ -269,10 +272,10 @@
     return jnp.sum(jnp.where(chosen, route_weights[:, :, None], 0.0), axis=1)
 
 
-def gathered(block, axis):
+def gathered(block, far_block, axis):
     size = lax.axis_size(axis)
-    parts = {0: block}
-    step = size // 2
+    parts = {0: block, size // 2: far_block}
+    step = size // 4
     while step:
         for k in sorted(parts):
             parts[k | step] = flip(parts[k], axis, step)
@@ -298,34 +301,40 @@
             [lax.dynamic_slice_in_dim(a, first, height, 0) for a in (hidden_in, grad_out)], axis=1
         )
         pieces.append(piece if step == 0 else flip(piece, "grp", step))
+    half_way = wide_size // 2
+    early = flip(pieces[0], "wide", half_way)
     ids = lax.dynamic_slice_in_dim(route_ids, place * height, height, 0)
     route = lax.dynamic_slice_in_dim(route_weights, place * height, height, 0)
     table = route_table(ids, route, local * wide_size)
     table = jnp.pad(table, ((0, 0), (0, LANES // 2 - table.shape[1])))
     high = table.astype(jnp.bfloat16)
     low = (table - high.astype(jnp.float32)).astype(jnp.bfloat16)
-    block = jnp.concatenate(pieces + [high, low], axis=1)
+    rest = jnp.concatenate(pieces[1:] + [high, low], axis=1)
+    far_block = jnp.concatenate([early, flip(rest, "wide", half_way)], axis=1)
+    block = jnp.concatenate([pieces[0], rest], axis=1)
     weights = load_weights(gate_proj, up_proj, down_proj, block, scalars)
-    blocks = gathered(block, "wide")
-    half_way = wide_size // 2
-    last = wide_size - 1
-    order = [k for k in range(1, wide_size)] + [0]
-    chunks = [order[i : i + half_way] for i in range(0, wide_size, half_way)]
+    blocks = gathered(block, far_block, "wide")
+    chunks = [list(range(first, wide_size, 2))[::-1] for first in (0, 1)]
     others = []
     for k in range(wide_size):
         others.append(flip(blocks[k], "rep", 1))
-    near = None
-    for chunk in chunks:
-        mine, other = chunk_gradient(
-            scalars, [blocks[k] for k in chunk], [others[k] for k in chunk], weights, groups
+    near, far = None, [[] for _ in range(groups // 2)]
+    for number, chunk in enumerate(chunks):
+        mine, other, *turned = chunk_gradient(
+            scalars,
+            [blocks[k] for k in chunk],
+            [others[k] for k in chunk],
+            weights,
+            groups,
+            turn=number == 0,
         )
+        weights = list(weights[:2]) + (turned or [weights[2]])
         swapped = flip(other, "rep", 1)
-        kinds = [(jnp.bfloat16 if k else jnp.float32, k == last) for k in chunk]
+        kinds = [(jnp.bfloat16 if k else jnp.float32, k == wide_size - 1) for k in chunk]
         for k, parts in zip(chunk, join(mine, swapped, kinds)):
-            if k == last:
-                far = []
+            if k == wide_size - 1:
                 for index, part in enumerate(parts):
-                    far.append(straight(part, k, index))
+                    far[index].append(straight(part, k, index))
                 continue
             part = parts[0]
             if k:
@@ -336,7 +345,9 @@
     keep, give = [], []
     for index in range(groups // 2):
         piece = straight(near[index].astype(jnp.bfloat16), 0, index)
-        piece = piece.astype(jnp.float32) + far[index].astype(jnp.float32)
+        piece = piece.astype(jnp.float32)
+        for part in far[index]:
+            piece = piece + part.astype(jnp.float32)
         piece = piece.astype(jnp.bfloat16)
         keep.append(jnp.where(first_core, piece[:height], piece[height:]))
         give.append(jnp.where(first_core, piece[height:], piece[:height]))

time: 70.5 us -> 68.6 us (0.973)
  starting transfers between devices: 22.3 us -> 20.4 us
    ppermute x4, waiting for transfers between devices: 3.26 us -> 4.7 us  [straight(): return lax.ppermute(array, ('wide', 'grp', 'rep'), pairs)]
    pallas_call x1, Pallas kernels: 8.43 us -> 7.07 us  [load_weights(): pl.pallas_call(load_kernel, in_specs=[HBM] * 3 + [VMEM, SMEM], out_specs=...]
    ppermute x4, starting transfers between devices: 6.07 us -> 5.03 us  [straight(): return lax.ppermute(array, ('wide', 'grp', 'rep'), pairs)]
    ppermute x15 -> x16, waiting for transfers between devices: 21.3 us -> 20.5 us  [flip(): return lax.ppermute(array, axis, [(i, i ^ step) for i in range(size)])]
    ppermute x15 -> x16, starting transfers between devices: 16.2 us -> 15.4 us  [flip(): return lax.ppermute(array, axis, [(i, i ^ step) for i in range(size)])]
  transfers between devices with their start and end apart: 19 -> 20, of which waited for: 9 -> 8; matrix products, arithmetic and copies ran while one was open for 1% -> 2% of each run, Pallas kernels for 29% -> 29%
where the time goes in v2:
time: 68.6 us; the launch traced here: 68.4 us
  waiting for transfers between devices  25.2 us (37%)
  starting transfers between devices  20.4 us (30%)
  Pallas kernels  19.7 us (29%)
  local copies, waits for them, and re-layouts  2.05 us (3%)
  other arithmetic  0.93 us (1%)
    ppermute x16, waiting for transfers between devices, flip(): return lax.ppermute(array, axis, [(i, i ^ step) for i in range(size)])  20.5 us
    ppermute x16, starting transfers between devices, flip(): return lax.ppermute(array, axis, [(i, i ^ step) for i in range(size)])  15.4 us
    pallas_call x2, Pallas kernels, chunk_gradient(): pl.pallas_call(lambda *refs: chunk_kernel(groups, 2 * slots, turn, *refs)...  12.5 us
    pallas_call x1, Pallas kernels, load_weights(): pl.pallas_call(load_kernel, in_specs=[HBM] * 3 + [VMEM, SMEM], out_specs=...  7.07 us
    ppermute x4, starting transfers between devices, straight(): return lax.ppermute(array, ('wide', 'grp', 'rep'), pairs)  5.03 us
    ppermute x4, waiting for transfers between devices, straight(): return lax.ppermute(array, ('wide', 'grp', 'rep'), pairs)  4.7 us
  transfers between devices with their start and end apart: 20, of which 8 were waited for; matrix products, arithmetic and copies ran while one was open for 2% of the time, Pallas kernels for 29%

profile of v2, /device:TPU:0, one launch (start us, length us, event | category | flops | bytes accessed | tf_op | source)
XLA Modules:
  0.0 68.4 jit_solution(7955766758827548957)
XLA Ops:
  0.0 0.0 copy-start
  0.0 0.9 %constant_dynamic-slice_fusion.2 = (bf16[32,512]{1,0:T(8,128)(2,1)S(1)}, bf16[32,512]{1,0:T(8,128)(2,1)S(1)}, bf16[32,512]{1,0:T(8,128)(2,1)S(1)}, bf16[32,512]{...) fusion(bf16[128,512]{1,0:T(8,128)(2,1)} %param.8, ...), kind=kLoop, calls=%fused_computation.31 | loop fusion | bytes 524304 | tf_op jit(solution)/shard_map/dynamic_slice | solution.py:301
  0.9 3.0 %collective-permute-start.1 = (bf16[32,1024]{1,0:T(8,128)(2,1)S(1)}, bf16[32,1024]{1,0:T(8,128)(2,1)S(1)}, u32[]{:S(2)}, u32[]{:S(2)}) collective-permute-start(bf16[32,1024]{1,0:T(8,128)(2,1)S(1)} %pad_maximum_fusion.2), channel_id=1, source_target_pairs={{0,2},{2,0},{4,6},{6,4},{1,3},{3,1},{5,7},{7,5},{8,10},{10,8},{12,... | collective-permute-start | bytes 196616 | tf_op jit(solution)/shard_map/ppermute | solution.py:256
  4.0 1.5 %collective-permute-start.2 = (bf16[32,1024]{1,0:T(8,128)(2,1)S(1)}, bf16[32,1024]{1,0:T(8,128)(2,1)S(1)}, u32[]{:S(2)}, u32[]{:S(2)}) collective-permute-start(bf16[32,1024]{1,0:T(8,128)(2,1)S(1)} %pad_maximum_fusion.3), channel_id=1, source_target_pairs={{0,4},{2,6},{4,0},{6,2},{1,5},{3,7},{5,1},{7,3},{8,12},{10,14},{12... | collective-permute-start | bytes 196616 | tf_op jit(solution)/shard_map/ppermute | solution.py:256
  5.5 0.1 collective-permute-start.3
  5.5 0.0 copy-done
  5.5 0.1 constant_dynamic-slice_fusion
  5.6 0.8 %constant_dynamic-slice_fusion.1 = s32[32,8]{0,1:T(8,128)S(1)} fusion(s32[128,8]{0,1:T(8,128)} %param.9, s32[]{:T(128)S(6)} %select_n.81), kind=kLoop, calls=%fused_computation.30 | loop fusion | bytes 2052 | tf_op jit(solution)/shard_map/dynamic_slice | solution.py:306
  6.4 0.1 copy.10
  6.5 0.0 collective-permute-done.1
  6.5 1.7 %collective-permute-done.2 = bf16[32,1024]{1,0:T(8,128)(2,1)S(1)} collective-permute-done((bf16[32,1024]{1,0:T(8,128)(2,1)S(1)}, bf16[32,1024]{1,0:T(8,128)(2,1)S(1)}, u32[]{:S(2)}, u32[]{:S(2)}) %collective-permute-start.2) | collective-permute-done | bytes 65568 | tf_op jit(solution)/shard_map/ppermute | solution.py:256
  8.2 2.4 %collective-permute-done.3 = bf16[32,1024]{1,0:T(8,128)(2,1)S(1)} collective-permute-done((bf16[32,1024]{1,0:T(8,128)(2,1)S(1)}, bf16[32,1024]{1,0:T(8,128)(2,1)S(1)}, u32[]{:S(2)}, u32[]{:S(2)}) %collective-permute-start.3) | collective-permute-done | bytes 65568 | tf_op jit(solution)/shard_map/ppermute | solution.py:256
  10.7 0.1 concatenate.32
  10.7 2.6 %collective-permute-start.4 = (bf16[32,3200]{1,0:T(8,128)(2,1)S(1)}, bf16[32,3200]{1,0:T(8,128)(2,1)S(1)}, u32[]{:S(2)}, u32[]{:S(2)}) collective-permute-start(bf16[32,3200]{1,0:T(8,128)(2,1)S(1)} %concatenate.32), channel_id=1, source_target_pairs={{0,16},{8,24},{16,0},{24,8},{1,17},{9,25},{17,1},{25,9},{2,18},{10... | collective-permute-start | bytes 614408 | tf_op jit(solution)/shard_map/ppermute | solution.py:256
  13.4 0.3 collective-permute-start
  13.7 0.1 concatenate.34.after.refs_2_
  13.8 1.6 %collective-permute-start.6 = (bf16[32,4224]{1,0:T(8,128)(2,1)S(1)}, bf16[32,4224]{1,0:T(8,128)(2,1)S(1)}, u32[]{:S(2)}, u32[]{:S(2)}) collective-permute-start(bf16[32,4224]{1,0:T(8,128)(2,1)S(1)} %concatenate.34.after.refs_2_), channel_id=1, source_target_pairs={{0,8},{8,0},{16,24},{24,16},{1,9},{9,1},{17,25},{25,17},{2,10},{10... | collective-permute-start | bytes 811016 | tf_op jit(solution)/shard_map/ppermute | solution.py:256
  15.5 8.6 %collective-permute-done = bf16[32,1024]{1,0:T(8,128)(2,1)S(1)} collective-permute-done((bf16[32,1024]{1,0:T(8,128)(2,1)S(1)}, bf16[32,1024]{1,0:T(8,128)(2,1)S(1)}, u32[]{:S(2)}, u32[]{:S(2)}) %collective-permute-start) | collective-permute-done | bytes 65568 | tf_op jit(solution)/shard_map/ppermute | solution.py:256
  24.1 0.0 collective-permute-done.4
  24.1 0.7 collective-permute-start.5
  24.8 0.0 collective-permute-start.10
  24.8 0.5 collective-permute-start.9
  25.3 0.1 pad_add_fusion.scalars.refs_0_
  25.4 7.1 %load.1 = (bf16[4,2048,768]{2,1,0:T(8,128)(2,1)S(1)}, bf16[4,768,2048]{2,1,0:T(8,128)(2,1)S(1)}, bf16[1536,2048]{1,0:T(8,128)(2,1)S(1)}) custom-call(bf16[4,2048,384]{2,1,0:T(8,128)(2,1)} %gate_hbm.1, bf16[4,2048,384]{2,1,0:T(8,128)(2,1)} %up_hbm.1, bf16[4,384,2048]{2,1,0:T(8,128)(2,1)} %down_hbm.1, bf16[32,4224]{1,0:T(8,128)(2,1)S(1)} %concatenate.34.after.refs_2_, ...), custom_call_target="tpu_custom_call" | custom-call | bytes 18874368 | tf_op jit(solution)/shard_map/load/pallas_call | solution.py:123
  32.5 0.0 collective-permute-done.6.refs_2_
  32.5 0.1 collective-permute-start.8
  32.6 0.0 collective-permute-done.5.refs_1_
  32.6 0.5 collective-permute-start.7
  33.1 0.0 collective-permute-done.10.refs_4_
  33.1 0.0 collective-permute-done.9.refs_3_
  33.1 6.4 %chunk.2 = (f32[2,2,64,512]{3,2,1,0:T(8,128)S(1)}, bf16[2,2,64,512]{3,2,1,0:T(8,128)(2,1)S(1)}, bf16[2048,1536]{1,0:T(8,128)(2,1)S(1)}) custom-call(s32[3]{0:T(128)S(1)} %pad_add_fusion.scalars.refs_0_, bf16[32,4224]{1,0:T(8,128)(2,1)S(1)} %constant_dynamic-update-slice_fusion.refs_1_, bf16[32,4224]{1,0:T(8,128)(2,1)S(1)} %concatenate.34.after.refs_2_, ...), custom_call_target="tpu_custom_call" | custom-call | flops 4026531840 | bytes 1048576 | tf_op jit(solution)/shard_map/chunk/pallas_call | solution.py:201
  39.5 0.2 collective-permute-start.13
  39.7 0.0 collective-permute-done.8.refs_4_
  39.7 0.0 collective-permute-done.7.refs_3_
  39.7 6.1 %chunk.3 = (f32[2,2,64,512]{3,2,1,0:T(8,128)S(1)}, bf16[2,2,64,512]{3,2,1,0:T(8,128)(2,1)S(1)}) custom-call(s32[3]{0:T(128)S(1)} %pad_add_fusion.scalars.refs_0_, bf16[32,4224]{1,0:T(8,128)(2,1)S(1)} %collective-permute-done.5.refs_1_, bf16[32,4224]{1,0:T(8,128)(2,1)S(1)} %collective-permute-done.6.refs_2_, ...), custom_call_target="tpu_custom_call" | custom-call | flops 4026531840 | bytes 1048576 | tf_op jit(solution)/shard_map/chunk/pallas_call | solution.py:201
  45.8 0.5 collective-permute-start.11
  46.3 0.0 collective-permute-done.13.refs_1_
  46.3 3.5 %collective-permute-start.14 = (bf16[2,64,512]{2,1,0:T(8,128)(2,1)S(1)}, bf16[2,64,512]{2,1,0:T(8,128)(2,1)S(1)}, u32[]{:S(2)}, u32[]{:S(2)}) collective-permute-start(bf16[2,64,512]{2,1,0:T(8,128)(2,1)S(1)} %get-tuple-element.28), channel_id=1, source_target_pairs={{0,16},{8,24},{16,0},{24,8},{1,17},{9,25},{17,1},{25,9},{2,18},{10... | collective-permute-start | bytes 393224 | tf_op jit(solution)/shard_map/ppermute | solution.py:256
  49.9 0.0 collective-permute-done.11.refs_1_
  49.9 0.2 collective-permute-start.12
  50.1 2.7 %collective-permute-start.16 = (bf16[64,512]{1,0:T(8,128)(2,1)S(1)}, bf16[64,512]{1,0:T(8,128)(2,1)S(1)}, u32[]{:S(2)}, u32[]{:S(2)}) collective-permute-start(bf16[64,512]{1,0:T(8,128)(2,1)S(1)} %get-tuple-element.29), channel_id=1, source_target_pairs={{0,26},{1,29},{2,24},{3,31},{4,30},{5,25},{6,28},{7,27},{8,18},{9,... | collective-permute-start | bytes 196616 | tf_op jit(solution)/shard_map/ppermute | solution.py:267
  52.8 4.1 %collective-permute-done.14 = bf16[2,64,512]{2,1,0:T(8,128)(2,1)S(1)} collective-permute-done((bf16[2,64,512]{2,1,0:T(8,128)(2,1)S(1)}, bf16[2,64,512]{2,1,0:T(8,128)(2,1)S(1)}, u32[]{:S(2)}, u32[]{:S(2)}) %collective-permute-start.14) | collective-permute-done | bytes 131104 | tf_op jit(solution)/shard_map/ppermute | solution.py:256
  56.9 2.3 %collective-permute-done.12 = bf16[2,64,512]{2,1,0:T(8,128)(2,1)S(1)} collective-permute-done((bf16[2,64,512]{2,1,0:T(8,128)(2,1)S(1)}, bf16[2,64,512]{2,1,0:T(8,128)(2,1)S(1)}, u32[]{:S(2)}, u32[]{:S(2)}) %collective-permute-start.12) | collective-permute-done | bytes 131104 | tf_op jit(solution)/shard_map/ppermute | solution.py:256
  59.3 1.0 %collective-permute-start.15 = (bf16[64,512]{1,0:T(8,128)(2,1)S(1)}, bf16[64,512]{1,0:T(8,128)(2,1)S(1)}, u32[]{:S(2)}, u32[]{:S(2)}) collective-permute-start(bf16[64,512]{1,0:T(8,128)(2,1)S(1)} %get-tuple-element.37), channel_id=1, source_target_pairs={{0,2},{1,5},{2,0},{3,7},{4,6},{5,1},{6,4},{7,3},{8,10},{9,13},{10,... | collective-permute-start | bytes 196616 | tf_op jit(solution)/shard_map/ppermute | solution.py:267
  60.3 0.7 collective-permute-start.18
  60.9 0.7 collective-permute-start.17
  61.6 0.0 collective-permute-done.16
  61.6 2.0 %collective-permute-done.15 = bf16[64,512]{1,0:T(8,128)(2,1)S(1)} collective-permute-done((bf16[64,512]{1,0:T(8,128)(2,1)S(1)}, bf16[64,512]{1,0:T(8,128)(2,1)S(1)}, u32[]{:S(2)}, u32[]{:S(2)}) %collective-permute-start.15) | collective-permute-done | bytes 65568 | tf_op jit(solution)/shard_map/ppermute | solution.py:267
  63.7 2.7 %collective-permute-done.18 = bf16[64,512]{1,0:T(8,128)(2,1)S(1)} collective-permute-done((bf16[64,512]{1,0:T(8,128)(2,1)S(1)}, bf16[64,512]{1,0:T(8,128)(2,1)S(1)}, u32[]{:S(2)}, u32[]{:S(2)}) %collective-permute-start.18) | collective-permute-done | bytes 65568 | tf_op jit(solution)/shard_map/ppermute | solution.py:267
  66.3 0.0 collective-permute-done.17
  66.4 0.1 collective-permute-start.19
  66.5 1.2 %collective-permute-done.19 = bf16[64,512]{1,0:T(8,128)(2,1)S(1)} collective-permute-done((bf16[64,512]{1,0:T(8,128)(2,1)S(1)}, bf16[64,512]{1,0:T(8,128)(2,1)S(1)}, u32[]{:S(2)}, u32[]{:S(2)}) %collective-permute-start.19) | collective-permute-done | bytes 65568 | tf_op jit(solution)/shard_map/ppermute | solution.py:256
  67.8 0.7 pad_maximum_fusion
  (20 shorter events, 0.3 us)
Async XLA Ops:
  0.0 5.5 %copy-start = (f32[128,8]{0,1:T(8,128)S(1)}, f32[128,8]{0,1:T(8,128)}, u32[]{:S(2)}) copy-start(f32[128,8]{0,1:T(8,128)} %param.10) | copy-start | bytes 12292
  0.9 5.6 %collective-permute-start.1 = (bf16[32,1024]{1,0:T(8,128)(2,1)S(1)}, bf16[32,1024]{1,0:T(8,128)(2,1)S(1)}, u32[]{:S(2)}, u32[]{:S(2)}) collective-permute-start(bf16[32,1024]{1,0:T(8,128)(2,1)S(1)} %pad_maximum_fusion.2), channel_id=1, source_target_pairs={{0,2},{2,0},{4,6},{6,4},{1,3},{3,1},{5,7},{7,5},{8,10},{10,8},{12,... | collective-permute-start | bytes 196616 | tf_op jit(solution)/shard_map/ppermute | solution.py:256
  4.0 4.3 %collective-permute-start.2 = (bf16[32,1024]{1,0:T(8,128)(2,1)S(1)}, bf16[32,1024]{1,0:T(8,128)(2,1)S(1)}, u32[]{:S(2)}, u32[]{:S(2)}) collective-permute-start(bf16[32,1024]{1,0:T(8,128)(2,1)S(1)} %pad_maximum_fusion.3), channel_id=1, source_target_pairs={{0,4},{2,6},{4,0},{6,2},{1,5},{3,7},{5,1},{7,3},{8,12},{10,14},{12... | collective-permute-start | bytes 196616 | tf_op jit(solution)/shard_map/ppermute | solution.py:256
  5.5 5.2 %collective-permute-start.3 = (bf16[32,1024]{1,0:T(8,128)(2,1)S(1)}, bf16[32,1024]{1,0:T(8,128)(2,1)S(1)}, u32[]{:S(2)}, u32[]{:S(2)}) collective-permute-start(bf16[32,1024]{1,0:T(8,128)(2,1)S(1)} %pad_maximum_fusion.4), channel_id=1, source_target_pairs={{0,6},{2,4},{4,2},{6,0},{1,7},{3,5},{5,3},{7,1},{8,14},{10,12},{12... | collective-permute-start | bytes 196616 | tf_op jit(solution)/shard_map/ppermute | solution.py:256
  10.7 13.4 %collective-permute-start.4 = (bf16[32,3200]{1,0:T(8,128)(2,1)S(1)}, bf16[32,3200]{1,0:T(8,128)(2,1)S(1)}, u32[]{:S(2)}, u32[]{:S(2)}) collective-permute-start(bf16[32,3200]{1,0:T(8,128)(2,1)S(1)} %concatenate.32), channel_id=1, source_target_pairs={{0,16},{8,24},{16,0},{24,8},{1,17},{9,25},{17,1},{25,9},{2,18},{10... | collective-permute-start | bytes 614408 | tf_op jit(solution)/shard_map/ppermute | solution.py:256
  13.4 10.7 %collective-permute-start = (bf16[32,1024]{1,0:T(8,128)(2,1)S(1)}, bf16[32,1024]{1,0:T(8,128)(2,1)S(1)}, u32[]{:S(2)}, u32[]{:S(2)}) collective-permute-start(bf16[32,1024]{1,0:T(8,128)(2,1)S(1)} %pad_maximum_fusion.1), channel_id=1, source_target_pairs={{0,16},{8,24},{16,0},{24,8},{1,17},{9,25},{17,1},{25,9},{2,18},{10... | collective-permute-start | bytes 196616 | tf_op jit(solution)/shard_map/ppermute | solution.py:256
  13.8 18.7 %collective-permute-start.6 = (bf16[32,4224]{1,0:T(8,128)(2,1)S(1)}, bf16[32,4224]{1,0:T(8,128)(2,1)S(1)}, u32[]{:S(2)}, u32[]{:S(2)}) collective-permute-start(bf16[32,4224]{1,0:T(8,128)(2,1)S(1)} %concatenate.34.after.refs_2_), channel_id=1, source_target_pairs={{0,8},{8,0},{16,24},{24,16},{1,9},{9,1},{17,25},{25,17},{2,10},{10... | collective-permute-start | bytes 811016 | tf_op jit(solution)/shard_map/ppermute | solution.py:256
  24.1 8.4 %collective-permute-start.5 = (bf16[32,4224]{1,0:T(8,128)(2,1)S(1)}, bf16[32,4224]{1,0:T(8,128)(2,1)S(1)}, u32[]{:S(2)}, u32[]{:S(2)}) collective-permute-start(bf16[32,4224]{1,0:T(8,128)(2,1)S(1)} %constant_dynamic-update-slice_fusion.refs_1_), channel_id=1, source_target_pairs={{0,8},{8,0},{16,24},{24,16},{1,9},{9,1},{17,25},{25,17},{2,10},{10... | collective-permute-start | bytes 811016 | tf_op jit(solution)/shard_map/ppermute | solution.py:256
  24.8 8.3 %collective-permute-start.10 = (bf16[32,4224]{1,0:T(8,128)(2,1)S(1)}, bf16[32,4224]{1,0:T(8,128)(2,1)S(1)}, u32[]{:S(2)}, u32[]{:S(2)}) collective-permute-start(bf16[32,4224]{1,0:T(8,128)(2,1)S(1)} %concatenate.34.after.refs_2_), channel_id=1, source_target_pairs={{0,1},{1,0},{2,3},{3,2},{4,5},{5,4},{6,7},{7,6},{8,9},{9,8},{10,11... | collective-permute-start | bytes 811016 | tf_op jit(solution)/shard_map/ppermute | solution.py:256
  24.8 8.3 %collective-permute-start.9 = (bf16[32,4224]{1,0:T(8,128)(2,1)S(1)}, bf16[32,4224]{1,0:T(8,128)(2,1)S(1)}, u32[]{:S(2)}, u32[]{:S(2)}) collective-permute-start(bf16[32,4224]{1,0:T(8,128)(2,1)S(1)} %constant_dynamic-update-slice_fusion.refs_1_), channel_id=1, source_target_pairs={{0,1},{1,0},{2,3},{3,2},{4,5},{5,4},{6,7},{7,6},{8,9},{9,8},{10,11... | collective-permute-start | bytes 811016 | tf_op jit(solution)/shard_map/ppermute | solution.py:256
  32.5 7.2 %collective-permute-start.8 = (bf16[32,4224]{1,0:T(8,128)(2,1)S(1)}, bf16[32,4224]{1,0:T(8,128)(2,1)S(1)}, u32[]{:S(2)}, u32[]{:S(2)}) collective-permute-start(bf16[32,4224]{1,0:T(8,128)(2,1)S(1)} %collective-permute-done.6.refs_2_), channel_id=1, source_target_pairs={{0,1},{1,0},{2,3},{3,2},{4,5},{5,4},{6,7},{7,6},{8,9},{9,8},{10,11... | collective-permute-start | bytes 811016 | tf_op jit(solution)/shard_map/ppermute | solution.py:256
  32.6 7.1 %collective-permute-start.7 = (bf16[32,4224]{1,0:T(8,128)(2,1)S(1)}, bf16[32,4224]{1,0:T(8,128)(2,1)S(1)}, u32[]{:S(2)}, u32[]{:S(2)}) collective-permute-start(bf16[32,4224]{1,0:T(8,128)(2,1)S(1)} %collective-permute-done.5.refs_1_), channel_id=1, source_target_pairs={{0,1},{1,0},{2,3},{3,2},{4,5},{5,4},{6,7},{7,6},{8,9},{9,8},{10,11... | collective-permute-start | bytes 811016 | tf_op jit(solution)/shard_map/ppermute | solution.py:256
  39.5 6.7 %collective-permute-start.13 = (bf16[2,2,64,512]{3,2,1,0:T(8,128)(2,1)S(1)}, bf16[2,2,64,512]{3,2,1,0:T(8,128)(2,1)S(1)}, u32[]{:S(2)}, u32[]{:S(2)}) collective-permute-start(bf16[2,2,64,512]{3,2,1,0:T(8,128)(2,1)S(1)} %get-tuple-element.26), channel_id=1, source_target_pairs={{0,1},{1,0},{2,3},{3,2},{4,5},{5,4},{6,7},{7,6},{8,9},{9,8},{10,11... | collective-permute-start | bytes 786440 | tf_op jit(solution)/shard_map/ppermute | solution.py:256
  45.8 4.1 %collective-permute-start.11 = (bf16[2,2,64,512]{3,2,1,0:T(8,128)(2,1)S(1)}, bf16[2,2,64,512]{3,2,1,0:T(8,128)(2,1)S(1)}, u32[]{:S(2)}, u32[]{:S(2)}) collective-permute-start(bf16[2,2,64,512]{3,2,1,0:T(8,128)(2,1)S(1)} %get-tuple-element.23), channel_id=1, source_target_pairs={{0,1},{1,0},{2,3},{3,2},{4,5},{5,4},{6,7},{7,6},{8,9},{9,8},{10,11... | collective-permute-start | bytes 786440 | tf_op jit(solution)/shard_map/ppermute | solution.py:256
  46.3 10.6 %collective-permute-start.14 = (bf16[2,64,512]{2,1,0:T(8,128)(2,1)S(1)}, bf16[2,64,512]{2,1,0:T(8,128)(2,1)S(1)}, u32[]{:S(2)}, u32[]{:S(2)}) collective-permute-start(bf16[2,64,512]{2,1,0:T(8,128)(2,1)S(1)} %get-tuple-element.28), channel_id=1, source_target_pairs={{0,16},{8,24},{16,0},{24,8},{1,17},{9,25},{17,1},{25,9},{2,18},{10... | collective-permute-start | bytes 393224 | tf_op jit(solution)/shard_map/ppermute | solution.py:256
  49.9 9.3 %collective-permute-start.12 = (bf16[2,64,512]{2,1,0:T(8,128)(2,1)S(1)}, bf16[2,64,512]{2,1,0:T(8,128)(2,1)S(1)}, u32[]{:S(2)}, u32[]{:S(2)}) collective-permute-start(bf16[2,64,512]{2,1,0:T(8,128)(2,1)S(1)} %get-tuple-element.24), channel_id=1, source_target_pairs={{0,8},{8,0},{16,24},{24,16},{1,9},{9,1},{17,25},{25,17},{2,10},{10... | collective-permute-start | bytes 393224 | tf_op jit(solution)/shard_map/ppermute | solution.py:256
  50.1 11.5 %collective-permute-start.16 = (bf16[64,512]{1,0:T(8,128)(2,1)S(1)}, bf16[64,512]{1,0:T(8,128)(2,1)S(1)}, u32[]{:S(2)}, u32[]{:S(2)}) collective-permute-start(bf16[64,512]{1,0:T(8,128)(2,1)S(1)} %get-tuple-element.29), channel_id=1, source_target_pairs={{0,26},{1,29},{2,24},{3,31},{4,30},{5,25},{6,28},{7,27},{8,18},{9,... | collective-permute-start | bytes 196616 | tf_op jit(solution)/shard_map/ppermute | solution.py:267
  59.3 4.3 %collective-permute-start.15 = (bf16[64,512]{1,0:T(8,128)(2,1)S(1)}, bf16[64,512]{1,0:T(8,128)(2,1)S(1)}, u32[]{:S(2)}, u32[]{:S(2)}) collective-permute-start(bf16[64,512]{1,0:T(8,128)(2,1)S(1)} %get-tuple-element.37), channel_id=1, source_target_pairs={{0,2},{1,5},{2,0},{3,7},{4,6},{5,1},{6,4},{7,3},{8,10},{9,13},{10,... | collective-permute-start | bytes 196616 | tf_op jit(solution)/shard_map/ppermute | solution.py:267
  60.3 6.1 %collective-permute-start.18 = (bf16[64,512]{1,0:T(8,128)(2,1)S(1)}, bf16[64,512]{1,0:T(8,128)(2,1)S(1)}, u32[]{:S(2)}, u32[]{:S(2)}) collective-permute-start(bf16[64,512]{1,0:T(8,128)(2,1)S(1)} %get-tuple-element.30), channel_id=1, source_target_pairs={{0,24},{1,31},{2,26},{3,29},{4,28},{5,27},{6,30},{7,25},{8,16},{9,... | collective-permute-start | bytes 196616 | tf_op jit(solution)/shard_map/ppermute | solution.py:267
  60.9 5.4 %collective-permute-start.17 = (bf16[64,512]{1,0:T(8,128)(2,1)S(1)}, bf16[64,512]{1,0:T(8,128)(2,1)S(1)}, u32[]{:S(2)}, u32[]{:S(2)}) collective-permute-start(bf16[64,512]{1,0:T(8,128)(2,1)S(1)} %get-tuple-element.38), channel_id=1, source_target_pairs={{0,0},{1,7},{2,2},{3,5},{4,4},{5,3},{6,6},{7,1},{8,8},{9,15},{10,1... | collective-permute-start | bytes 196616 | tf_op jit(solution)/shard_map/ppermute | solution.py:267
  66.4 1.3 %collective-permute-start.19 = (bf16[64,512]{1,0:T(8,128)(2,1)S(1)}, bf16[64,512]{1,0:T(8,128)(2,1)S(1)}, u32[]{:S(2)}, u32[]{:S(2)}) collective-permute-start(bf16[64,512]{1,0:T(8,128)(2,1)S(1)} %pad_maximum_fusion.5), channel_id=1, source_target_pairs={{0,1},{1,0},{2,3},{3,2},{4,5},{5,4},{6,7},{7,6},{8,9},{9,8},{10,11... | collective-permute-start | bytes 196616 | tf_op jit(solution)/shard_map/ppermute | solution.py:256

commit v3 on v2

--- a/solution.py
+++ b/solution.py
@@ -140,9 +140,9 @@
     place, wide = scalars[0], scalars[1]
     blocks = refs[:count]
     if turn:
-        both, both_t, down, mine_out, other_out, down_t, x_rows, g_rows, total = refs[count:]
+        both, both_t, down, hidden_out, give_out, down_t, x_rows, g_rows, total = refs[count:]
     else:
-        both, both_t, down_t, mine_out, other_out, x_rows, g_rows, total = refs[count:]
+        both, both_t, down_t, hidden_out, give_out, x_rows, g_rows, total = refs[count:]
     local, width, double = both.shape
     half = double // 2
     height = blocks[0].shape[0]
@@ -177,20 +177,58 @@
         d_gate = back * pre_up * sig * (1.0 + pre_gate * (1.0 - sig))
         d_up = back * pre_gate * sig
         hidden = jnp.concatenate([d_gate, d_up], axis=1).astype(jnp.bfloat16)
-        term = jnp.dot(hidden, both_t[e], preferred_element_type=jnp.float32)
+        hidden_out[e] = hidden
+        add_places(scalars, 1 - scalars[2], hidden, both_t, e, total)
+    put_places(scalars, total, give_out)
+
+
+def add_places(scalars, core, hidden, both_t, e, total):
+    cols = total.shape[2]
+    groups = both_t.shape[2] // cols
+    for index in range(total.shape[0]):
+        start = (scalars[0] ^ (core * (groups - 1)) ^ index) * cols
+        columns = pl.ds(pl.multiple_of(start, LANES), cols)
+        term = jnp.dot(hidden, both_t[e, :, columns], preferred_element_type=jnp.float32)
         if e == 0:
-            total[...] = term
+            total[index] = term
         else:
-            total[...] += term
-    slots = count // 2
-    for out, core in ((mine_out, scalars[2]), (other_out, 1 - scalars[2])):
-        for index in range(groups // 2):
-            start = pl.multiple_of((place ^ (core * (groups - 1)) ^ index) * cols, LANES)
-            for slot in range(slots):
-                for rep in range(2):
-                    first = ((scalars[2] ^ rep) * slots + slot) * height
-                    part = total[pl.ds(pl.multiple_of(first, height), height), pl.ds(start, cols)]
-                    out[slot, index, rep * height : (rep + 1) * height, :] = part.astype(out.dtype)
+            total[index] += term
+
+
+def put_places(scalars, total, out):
+    slots, _, double, _ = out.shape
+    height = double // 2
+    for index in range(total.shape[0]):
+        for slot in range(slots):
+            for rep in range(2):
+                first = pl.multiple_of(((scalars[2] ^ rep) * slots + slot) * height, height)
+                part = total[index, pl.ds(first, height), :]
+                out[slot, index, rep * height : (rep + 1) * height, :] = part.astype(out.dtype)
+
+
+def keep_kernel(scalars, hidden, both_t, keep_out, total):
+    for e in range(hidden.shape[0]):
+        add_places(scalars, scalars[2], hidden[e], both_t, e, total)
+    put_places(scalars, total, keep_out)
+
+
+def keep_gradient(scalars, hidden, both_t, give):
+    local, rows, double = hidden.shape
+    _, places, _, cols = give.shape
+    return pl.pallas_call(
+        keep_kernel,
+        in_specs=[SMEM] + [VMEM] * 2,
+        out_specs=VMEM,
+        out_shape=jax.ShapeDtypeStruct(give.shape, jnp.float32),
+        scratch_shapes=[pltpu.VMEM((places, rows, cols), jnp.float32)],
+        compiler_params=pltpu.CompilerParams(vmem_limit_bytes=16 * rows * places * cols),
+        cost_estimate=pl.CostEstimate(
+            flops=2 * rows * double * places * cols * local,
+            bytes_accessed=2 * local * rows * double,
+            transcendentals=0,
+        ),
+        name="keep",
+    )(scalars, hidden, both_t)
 
 
 def chunk_gradient(scalars, mine, other, weights, groups, turn):
@@ -203,14 +241,14 @@
         in_specs=[SMEM] + [VMEM] * (2 * slots + 3),
         out_specs=[VMEM] * (3 if turn else 2),
         out_shape=[
-            jax.ShapeDtypeStruct(shape, jnp.float32),
+            jax.ShapeDtypeStruct((local, rows, double), jnp.bfloat16),
             jax.ShapeDtypeStruct(shape, jnp.bfloat16),
         ]
         + [jax.ShapeDtypeStruct(weights[2].shape[::-1], jnp.bfloat16)] * turn,
         scratch_shapes=[
             pltpu.VMEM((rows, width), jnp.bfloat16),
             pltpu.VMEM((rows, width), jnp.bfloat16),
-            pltpu.VMEM((rows, width), jnp.float32),
+            pltpu.VMEM((groups // 2, rows, width // groups), jnp.float32),
         ],
         compiler_params=pltpu.CompilerParams(vmem_limit_bytes=16 * rows * width),
         cost_estimate=pl.CostEstimate(
@@ -320,7 +358,7 @@
         others.append(flip(blocks[k], "rep", 1))
     near, far = None, [[] for _ in range(groups // 2)]
     for number, chunk in enumerate(chunks):
-        mine, other, *turned = chunk_gradient(
+        hidden, give, *turned = chunk_gradient(
             scalars,
             [blocks[k] for k in chunk],
             [others[k] for k in chunk],
@@ -329,7 +367,8 @@
             turn=number == 0,
         )
         weights = list(weights[:2]) + (turned or [weights[2]])
-        swapped = flip(other, "rep", 1)
+        swapped = flip(give, "rep", 1)
+        mine = keep_gradient(scalars, hidden, weights[1], give)
         kinds = [(jnp.bfloat16 if k else jnp.float32, k == wide_size - 1) for k in chunk]
         for k, parts in zip(chunk, join(mine, swapped, kinds)):
             if k == wide_size - 1:

time: 68.6 us -> 70.3 us (1.025)
  waiting for transfers between devices: 25.2 us -> 27 us
  starting transfers between devices: 20.4 us -> 18.7 us
  Pallas kernels: 19.7 us -> 21.2 us
    pallas_call x0 -> x2, Pallas kernels: none -> 3.21 us  [keep_gradient(): pl.pallas_call(keep_kernel, in_specs=[SMEM] + [VMEM] * 2, out_specs=VMEM,...]
    pallas_call x2, Pallas kernels: 12.5 us -> 10.8 us  [chunk_gradient(): pl.pallas_call(lambda *refs: chunk_kernel(groups, 2 * slots, turn, *refs)...]
    ppermute x4, starting transfers between devices: 5.03 us -> 3.35 us  [straight(): return lax.ppermute(array, ('wide', 'grp', 'rep'), pairs)]
    ppermute x4, waiting for transfers between devices: 4.7 us -> 5.72 us  [straight(): return lax.ppermute(array, ('wide', 'grp', 'rep'), pairs)]
    ppermute x16, waiting for transfers between devices: 20.5 us -> 21.3 us  [flip(): return lax.ppermute(array, axis, [(i, i ^ step) for i in range(size)])]
  transfers between devices with their start and end apart: 20 -> 20, of which waited for: 8 -> 8; matrix products, arithmetic and copies ran while one was open for 2% -> 2% of each run, Pallas kernels for 29% -> 30%
where the time goes in v3:
time: 70.3 us; the launch traced here: 70.1 us
  waiting for transfers between devices  27 us (38%)
  Pallas kernels  21.2 us (30%)
  starting transfers between devices  18.7 us (27%)
  local copies, waits for them, and re-layouts  2.05 us (3%)
  other arithmetic  0.93 us (1%)
    ppermute x16, waiting for transfers between devices, flip(): return lax.ppermute(array, axis, [(i, i ^ step) for i in range(size)])  21.3 us
    ppermute x16, starting transfers between devices, flip(): return lax.ppermute(array, axis, [(i, i ^ step) for i in range(size)])  15.4 us
    pallas_call x2, Pallas kernels, chunk_gradient(): pl.pallas_call(lambda *refs: chunk_kernel(groups, 2 * slots, turn, *refs)...  10.8 us
    pallas_call x1, Pallas kernels, load_weights(): pl.pallas_call(load_kernel, in_specs=[HBM] * 3 + [VMEM, SMEM], out_specs=...  7.07 us
    ppermute x4, waiting for transfers between devices, straight(): return lax.ppermute(array, ('wide', 'grp', 'rep'), pairs)  5.72 us
    ppermute x4, starting transfers between devices, straight(): return lax.ppermute(array, ('wide', 'grp', 'rep'), pairs)  3.35 us
    pallas_call x2, Pallas kernels, keep_gradient(): pl.pallas_call(keep_kernel, in_specs=[SMEM] + [VMEM] * 2, out_specs=VMEM,...  3.21 us
  transfers between devices with their start and end apart: 20, of which 8 were waited for; matrix products, arithmetic and copies ran while one was open for 2% of the time, Pallas kernels for 30%

profile of v3, /device:TPU:0, one launch (start us, length us, event | category | flops | bytes accessed | tf_op | source)
XLA Modules:
  0.0 70.1 jit_solution(14581801596961806463)
XLA Ops:
  0.0 0.0 copy-start
  0.0 0.9 %constant_dynamic-slice_fusion.2 = (bf16[32,512]{1,0:T(8,128)(2,1)S(1)}, bf16[32,512]{1,0:T(8,128)(2,1)S(1)}, bf16[32,512]{1,0:T(8,128)(2,1)S(1)}, bf16[32,512]{...) fusion(bf16[128,512]{1,0:T(8,128)(2,1)} %param.8, ...), kind=kLoop, calls=%fused_computation.31 | loop fusion | bytes 524304 | tf_op jit(solution)/shard_map/dynamic_slice | solution.py:339
  0.9 3.0 %collective-permute-start.1 = (bf16[32,1024]{1,0:T(8,128)(2,1)S(1)}, bf16[32,1024]{1,0:T(8,128)(2,1)S(1)}, u32[]{:S(2)}, u32[]{:S(2)}) collective-permute-start(bf16[32,1024]{1,0:T(8,128)(2,1)S(1)} %pad_maximum_fusion.2), channel_id=1, source_target_pairs={{0,2},{2,0},{4,6},{6,4},{1,3},{3,1},{5,7},{7,5},{8,10},{10,8},{12,... | collective-permute-start | bytes 196616 | tf_op jit(solution)/shard_map/ppermute | solution.py:294
  4.0 1.5 %collective-permute-start.2 = (bf16[32,1024]{1,0:T(8,128)(2,1)S(1)}, bf16[32,1024]{1,0:T(8,128)(2,1)S(1)}, u32[]{:S(2)}, u32[]{:S(2)}) collective-permute-start(bf16[32,1024]{1,0:T(8,128)(2,1)S(1)} %pad_maximum_fusion.3), channel_id=1, source_target_pairs={{0,4},{2,6},{4,0},{6,2},{1,5},{3,7},{5,1},{7,3},{8,12},{10,14},{12... | collective-permute-start | bytes 196616 | tf_op jit(solution)/shard_map/ppermute | solution.py:294
  5.5 0.1 collective-permute-start.3
  5.5 0.0 copy-done
  5.5 0.1 constant_dynamic-slice_fusion
  5.6 0.8 %constant_dynamic-slice_fusion.1 = s32[32,8]{0,1:T(8,128)S(1)} fusion(s32[128,8]{0,1:T(8,128)} %param.9, s32[]{:T(128)S(6)} %select_n.81), kind=kLoop, calls=%fused_computation.30 | loop fusion | bytes 2052 | tf_op jit(solution)/shard_map/dynamic_slice | solution.py:344
  6.4 0.1 copy.10
  6.5 0.0 collective-permute-done.1
  6.5 1.7 %collective-permute-done.2 = bf16[32,1024]{1,0:T(8,128)(2,1)S(1)} collective-permute-done((bf16[32,1024]{1,0:T(8,128)(2,1)S(1)}, bf16[32,1024]{1,0:T(8,128)(2,1)S(1)}, u32[]{:S(2)}, u32[]{:S(2)}) %collective-permute-start.2) | collective-permute-done | bytes 65568 | tf_op jit(solution)/shard_map/ppermute | solution.py:294
  8.2 2.4 %collective-permute-done.3 = bf16[32,1024]{1,0:T(8,128)(2,1)S(1)} collective-permute-done((bf16[32,1024]{1,0:T(8,128)(2,1)S(1)}, bf16[32,1024]{1,0:T(8,128)(2,1)S(1)}, u32[]{:S(2)}, u32[]{:S(2)}) %collective-permute-start.3) | collective-permute-done | bytes 65568 | tf_op jit(solution)/shard_map/ppermute | solution.py:294
  10.7 0.1 concatenate.32
  10.7 2.6 %collective-permute-start.4 = (bf16[32,3200]{1,0:T(8,128)(2,1)S(1)}, bf16[32,3200]{1,0:T(8,128)(2,1)S(1)}, u32[]{:S(2)}, u32[]{:S(2)}) collective-permute-start(bf16[32,3200]{1,0:T(8,128)(2,1)S(1)} %concatenate.32), channel_id=1, source_target_pairs={{0,16},{8,24},{16,0},{24,8},{1,17},{9,25},{17,1},{25,9},{2,18},{10... | collective-permute-start | bytes 614408 | tf_op jit(solution)/shard_map/ppermute | solution.py:294
  13.4 0.3 collective-permute-start
  13.7 0.1 concatenate.34.after.refs_2_
  13.8 1.6 %collective-permute-start.6 = (bf16[32,4224]{1,0:T(8,128)(2,1)S(1)}, bf16[32,4224]{1,0:T(8,128)(2,1)S(1)}, u32[]{:S(2)}, u32[]{:S(2)}) collective-permute-start(bf16[32,4224]{1,0:T(8,128)(2,1)S(1)} %concatenate.34.after.refs_2_), channel_id=1, source_target_pairs={{0,8},{8,0},{16,24},{24,16},{1,9},{9,1},{17,25},{25,17},{2,10},{10... | collective-permute-start | bytes 811016 | tf_op jit(solution)/shard_map/ppermute | solution.py:294
  15.5 8.6 %collective-permute-done = bf16[32,1024]{1,0:T(8,128)(2,1)S(1)} collective-permute-done((bf16[32,1024]{1,0:T(8,128)(2,1)S(1)}, bf16[32,1024]{1,0:T(8,128)(2,1)S(1)}, u32[]{:S(2)}, u32[]{:S(2)}) %collective-permute-start) | collective-permute-done | bytes 65568 | tf_op jit(solution)/shard_map/ppermute | solution.py:294
  24.1 0.0 collective-permute-done.4
  24.1 0.7 collective-permute-start.5
  24.8 0.0 collective-permute-start.10
  24.8 0.5 collective-permute-start.9
  25.3 0.1 pad_add_fusion.scalars.refs_0_
  25.4 7.1 %load.1 = (bf16[4,2048,768]{2,1,0:T(8,128)(2,1)S(1)}, bf16[4,768,2048]{2,1,0:T(8,128)(2,1)S(1)}, bf16[1536,2048]{1,0:T(8,128)(2,1)S(1)}) custom-call(bf16[4,2048,384]{2,1,0:T(8,128)(2,1)} %gate_hbm.1, bf16[4,2048,384]{2,1,0:T(8,128)(2,1)} %up_hbm.1, bf16[4,384,2048]{2,1,0:T(8,128)(2,1)} %down_hbm.1, bf16[32,4224]{1,0:T(8,128)(2,1)S(1)} %concatenate.34.after.refs_2_, ...), custom_call_target="tpu_custom_call" | custom-call | bytes 18874368 | tf_op jit(solution)/shard_map/load/pallas_call | solution.py:123
  32.5 0.0 collective-permute-done.6.refs_2_
  32.5 0.1 collective-permute-start.8
  32.6 0.0 collective-permute-done.5.refs_1_
  32.6 0.5 collective-permute-start.7
  33.1 0.0 collective-permute-done.10.refs_4_
  33.1 0.0 collective-permute-done.9.refs_3_
  33.1 5.6 %chunk.2 = (bf16[4,128,768]{2,1,0:T(8,128)(2,1)S(1)}, bf16[2,2,64,512]{3,2,1,0:T(8,128)(2,1)S(1)}, bf16[2048,1536]{1,0:T(8,128)(2,1)S(1)}) custom-call(s32[3]{0:T(128)S(1)} %pad_add_fusion.scalars.refs_0_, bf16[32,4224]{1,0:T(8,128)(2,1)S(1)} %constant_dynamic-update-slice_fusion.refs_1_, bf16[32,4224]{1,0:T(8,128)(2,1)S(1)} %concatenate.34.after.refs_2_, ...), custom_call_target="tpu_custom_call" | custom-call | flops 4026531840 | bytes 1048576 | tf_op jit(solution)/shard_map/chunk/pallas_call | solution.py:239
  38.7 0.2 collective-permute-start.13
  38.9 0.0 collective-permute-done.8.refs_4_
  38.9 0.0 collective-permute-done.7.refs_3_
  38.9 5.2 %chunk.3 = (bf16[4,128,768]{2,1,0:T(8,128)(2,1)S(1)}, bf16[2,2,64,512]{3,2,1,0:T(8,128)(2,1)S(1)}) custom-call(s32[3]{0:T(128)S(1)} %pad_add_fusion.scalars.refs_0_, bf16[32,4224]{1,0:T(8,128)(2,1)S(1)} %collective-permute-done.5.refs_1_, bf16[32,4224]{1,0:T(8,128)(2,1)S(1)} %collective-permute-done.6.refs_2_, ...), custom_call_target="tpu_custom_call" | custom-call | flops 4026531840 | bytes 1048576 | tf_op jit(solution)/shard_map/chunk/pallas_call | solution.py:239
  44.1 0.5 collective-permute-start.11
  44.6 1.6 %keep.3.refs_0_ = f32[2,2,64,512]{3,2,1,0:T(8,128)S(1)} custom-call(s32[3]{0:T(128)S(1)} %pad_add_fusion.scalars.refs_0_, bf16[4,128,768]{2,1,0:T(8,128)(2,1)S(1)} %get-tuple-element.25.hidden, bf16[4,768,2048]{2,1,0:T(8,128)(2,1)S(1)} %get-tuple-element.19.refs_6_.both_t), custom_call_target="tpu_custom_call" | custom-call | flops 805306368 | bytes 786432 | tf_op jit(solution)/shard_map/keep/pallas_call | solution.py:218
  46.2 0.0 collective-permute-done.13.refs_1_
  46.3 3.5 %collective-permute-start.14 = (bf16[2,64,512]{2,1,0:T(8,128)(2,1)S(1)}, bf16[2,64,512]{2,1,0:T(8,128)(2,1)S(1)}, u32[]{:S(2)}, u32[]{:S(2)}) collective-permute-start(bf16[2,64,512]{2,1,0:T(8,128)(2,1)S(1)} %get-tuple-element.28), channel_id=1, source_target_pairs={{0,16},{8,24},{16,0},{24,8},{1,17},{9,25},{17,1},{25,9},{2,18},{10... | collective-permute-start | bytes 393224 | tf_op jit(solution)/shard_map/ppermute | solution.py:294
  49.8 1.6 %keep.2.refs_0_ = f32[2,2,64,512]{3,2,1,0:T(8,128)S(1)} custom-call(s32[3]{0:T(128)S(1)} %pad_add_fusion.scalars.refs_0_, bf16[4,128,768]{2,1,0:T(8,128)(2,1)S(1)} %get-tuple-element.22.hidden, bf16[4,768,2048]{2,1,0:T(8,128)(2,1)S(1)} %get-tuple-element.19.refs_6_.both_t), custom_call_target="tpu_custom_call" | custom-call | flops 805306368 | bytes 786432 | tf_op jit(solution)/shard_map/keep/pallas_call | solution.py:218
  51.4 0.0 collective-permute-done.11.refs_1_
  51.4 0.2 collective-permute-start.12
  51.6 1.7 %collective-permute-start.16 = (bf16[64,512]{1,0:T(8,128)(2,1)S(1)}, bf16[64,512]{1,0:T(8,128)(2,1)S(1)}, u32[]{:S(2)}, u32[]{:S(2)}) collective-permute-start(bf16[64,512]{1,0:T(8,128)(2,1)S(1)} %get-tuple-element.29), channel_id=1, source_target_pairs={{0,26},{1,29},{2,24},{3,31},{4,30},{5,25},{6,28},{7,27},{8,18},{9,... | collective-permute-start | bytes 196616 | tf_op jit(solution)/shard_map/ppermute | solution.py:305
  53.3 3.7 %collective-permute-done.14 = bf16[2,64,512]{2,1,0:T(8,128)(2,1)S(1)} collective-permute-done((bf16[2,64,512]{2,1,0:T(8,128)(2,1)S(1)}, bf16[2,64,512]{2,1,0:T(8,128)(2,1)S(1)}, u32[]{:S(2)}, u32[]{:S(2)}) %collective-permute-start.14) | collective-permute-done | bytes 131104 | tf_op jit(solution)/shard_map/ppermute | solution.py:294
  57.1 3.5 %collective-permute-done.12 = bf16[2,64,512]{2,1,0:T(8,128)(2,1)S(1)} collective-permute-done((bf16[2,64,512]{2,1,0:T(8,128)(2,1)S(1)}, bf16[2,64,512]{2,1,0:T(8,128)(2,1)S(1)}, u32[]{:S(2)}, u32[]{:S(2)}) %collective-permute-start.12) | collective-permute-done | bytes 131104 | tf_op jit(solution)/shard_map/ppermute | solution.py:294
  60.6 1.0 %collective-permute-start.15 = (bf16[64,512]{1,0:T(8,128)(2,1)S(1)}, bf16[64,512]{1,0:T(8,128)(2,1)S(1)}, u32[]{:S(2)}, u32[]{:S(2)}) collective-permute-start(bf16[64,512]{1,0:T(8,128)(2,1)S(1)} %get-tuple-element.37), channel_id=1, source_target_pairs={{0,2},{1,5},{2,0},{3,7},{4,6},{5,1},{6,4},{7,3},{8,10},{9,13},{10,... | collective-permute-start | bytes 196616 | tf_op jit(solution)/shard_map/ppermute | solution.py:305
  61.6 0.0 collective-permute-start.18
  61.6 0.7 collective-permute-start.17
  62.2 0.0 collective-permute-done.16
  62.3 2.7 %collective-permute-done.15 = bf16[64,512]{1,0:T(8,128)(2,1)S(1)} collective-permute-done((bf16[64,512]{1,0:T(8,128)(2,1)S(1)}, bf16[64,512]{1,0:T(8,128)(2,1)S(1)}, u32[]{:S(2)}, u32[]{:S(2)}) %collective-permute-start.15) | collective-permute-done | bytes 65568 | tf_op jit(solution)/shard_map/ppermute | solution.py:305
  65.0 3.0 %collective-permute-done.18 = bf16[64,512]{1,0:T(8,128)(2,1)S(1)} collective-permute-done((bf16[64,512]{1,0:T(8,128)(2,1)S(1)}, bf16[64,512]{1,0:T(8,128)(2,1)S(1)}, u32[]{:S(2)}, u32[]{:S(2)}) %collective-permute-start.18) | collective-permute-done | bytes 65568 | tf_op jit(solution)/shard_map/ppermute | solution.py:305
  68.0 0.0 collective-permute-done.17
  68.1 0.1 collective-permute-start.19
  68.2 1.2 %collective-permute-done.19 = bf16[64,512]{1,0:T(8,128)(2,1)S(1)} collective-permute-done((bf16[64,512]{1,0:T(8,128)(2,1)S(1)}, bf16[64,512]{1,0:T(8,128)(2,1)S(1)}, u32[]{:S(2)}, u32[]{:S(2)}) %collective-permute-start.19) | collective-permute-done | bytes 65568 | tf_op jit(solution)/shard_map/ppermute | solution.py:294
  69.4 0.7 pad_maximum_fusion
  (20 shorter events, 0.3 us)
Async XLA Ops:
  0.0 5.5 %copy-start = (f32[128,8]{0,1:T(8,128)S(1)}, f32[128,8]{0,1:T(8,128)}, u32[]{:S(2)}) copy-start(f32[128,8]{0,1:T(8,128)} %param.10) | copy-start | bytes 12292
  0.9 5.6 %collective-permute-start.1 = (bf16[32,1024]{1,0:T(8,128)(2,1)S(1)}, bf16[32,1024]{1,0:T(8,128)(2,1)S(1)}, u32[]{:S(2)}, u32[]{:S(2)}) collective-permute-start(bf16[32,1024]{1,0:T(8,128)(2,1)S(1)} %pad_maximum_fusion.2), channel_id=1, source_target_pairs={{0,2},{2,0},{4,6},{6,4},{1,3},{3,1},{5,7},{7,5},{8,10},{10,8},{12,... | collective-permute-start | bytes 196616 | tf_op jit(solution)/shard_map/ppermute | solution.py:294
  4.0 4.3 %collective-permute-start.2 = (bf16[32,1024]{1,0:T(8,128)(2,1)S(1)}, bf16[32,1024]{1,0:T(8,128)(2,1)S(1)}, u32[]{:S(2)}, u32[]{:S(2)}) collective-permute-start(bf16[32,1024]{1,0:T(8,128)(2,1)S(1)} %pad_maximum_fusion.3), channel_id=1, source_target_pairs={{0,4},{2,6},{4,0},{6,2},{1,5},{3,7},{5,1},{7,3},{8,12},{10,14},{12... | collective-permute-start | bytes 196616 | tf_op jit(solution)/shard_map/ppermute | solution.py:294
  5.5 5.2 %collective-permute-start.3 = (bf16[32,1024]{1,0:T(8,128)(2,1)S(1)}, bf16[32,1024]{1,0:T(8,128)(2,1)S(1)}, u32[]{:S(2)}, u32[]{:S(2)}) collective-permute-start(bf16[32,1024]{1,0:T(8,128)(2,1)S(1)} %pad_maximum_fusion.4), channel_id=1, source_target_pairs={{0,6},{2,4},{4,2},{6,0},{1,7},{3,5},{5,3},{7,1},{8,14},{10,12},{12... | collective-permute-start | bytes 196616 | tf_op jit(solution)/shard_map/ppermute | solution.py:294
  10.7 13.4 %collective-permute-start.4 = (bf16[32,3200]{1,0:T(8,128)(2,1)S(1)}, bf16[32,3200]{1,0:T(8,128)(2,1)S(1)}, u32[]{:S(2)}, u32[]{:S(2)}) collective-permute-start(bf16[32,3200]{1,0:T(8,128)(2,1)S(1)} %concatenate.32), channel_id=1, source_target_pairs={{0,16},{8,24},{16,0},{24,8},{1,17},{9,25},{17,1},{25,9},{2,18},{10... | collective-permute-start | bytes 614408 | tf_op jit(solution)/shard_map/ppermute | solution.py:294
  13.4 10.7 %collective-permute-start = (bf16[32,1024]{1,0:T(8,128)(2,1)S(1)}, bf16[32,1024]{1,0:T(8,128)(2,1)S(1)}, u32[]{:S(2)}, u32[]{:S(2)}) collective-permute-start(bf16[32,1024]{1,0:T(8,128)(2,1)S(1)} %pad_maximum_fusion.1), channel_id=1, source_target_pairs={{0,16},{8,24},{16,0},{24,8},{1,17},{9,25},{17,1},{25,9},{2,18},{10... | collective-permute-start | bytes 196616 | tf_op jit(solution)/shard_map/ppermute | solution.py:294
  13.8 18.7 %collective-permute-start.6 = (bf16[32,4224]{1,0:T(8,128)(2,1)S(1)}, bf16[32,4224]{1,0:T(8,128)(2,1)S(1)}, u32[]{:S(2)}, u32[]{:S(2)}) collective-permute-start(bf16[32,4224]{1,0:T(8,128)(2,1)S(1)} %concatenate.34.after.refs_2_), channel_id=1, source_target_pairs={{0,8},{8,0},{16,24},{24,16},{1,9},{9,1},{17,25},{25,17},{2,10},{10... | collective-permute-start | bytes 811016 | tf_op jit(solution)/shard_map/ppermute | solution.py:294
  24.1 8.4 %collective-permute-start.5 = (bf16[32,4224]{1,0:T(8,128)(2,1)S(1)}, bf16[32,4224]{1,0:T(8,128)(2,1)S(1)}, u32[]{:S(2)}, u32[]{:S(2)}) collective-permute-start(bf16[32,4224]{1,0:T(8,128)(2,1)S(1)} %constant_dynamic-update-slice_fusion.refs_1_), channel_id=1, source_target_pairs={{0,8},{8,0},{16,24},{24,16},{1,9},{9,1},{17,25},{25,17},{2,10},{10... | collective-permute-start | bytes 811016 | tf_op jit(solution)/shard_map/ppermute | solution.py:294
  24.8 8.3 %collective-permute-start.10 = (bf16[32,4224]{1,0:T(8,128)(2,1)S(1)}, bf16[32,4224]{1,0:T(8,128)(2,1)S(1)}, u32[]{:S(2)}, u32[]{:S(2)}) collective-permute-start(bf16[32,4224]{1,0:T(8,128)(2,1)S(1)} %concatenate.34.after.refs_2_), channel_id=1, source_target_pairs={{0,1},{1,0},{2,3},{3,2},{4,5},{5,4},{6,7},{7,6},{8,9},{9,8},{10,11... | collective-permute-start | bytes 811016 | tf_op jit(solution)/shard_map/ppermute | solution.py:294
  24.8 8.3 %collective-permute-start.9 = (bf16[32,4224]{1,0:T(8,128)(2,1)S(1)}, bf16[32,4224]{1,0:T(8,128)(2,1)S(1)}, u32[]{:S(2)}, u32[]{:S(2)}) collective-permute-start(bf16[32,4224]{1,0:T(8,128)(2,1)S(1)} %constant_dynamic-update-slice_fusion.refs_1_), channel_id=1, source_target_pairs={{0,1},{1,0},{2,3},{3,2},{4,5},{5,4},{6,7},{7,6},{8,9},{9,8},{10,11... | collective-permute-start | bytes 811016 | tf_op jit(solution)/shard_map/ppermute | solution.py:294
  32.5 6.4 %collective-permute-start.8 = (bf16[32,4224]{1,0:T(8,128)(2,1)S(1)}, bf16[32,4224]{1,0:T(8,128)(2,1)S(1)}, u32[]{:S(2)}, u32[]{:S(2)}) collective-permute-start(bf16[32,4224]{1,0:T(8,128)(2,1)S(1)} %collective-permute-done.6.refs_2_), channel_id=1, source_target_pairs={{0,1},{1,0},{2,3},{3,2},{4,5},{5,4},{6,7},{7,6},{8,9},{9,8},{10,11... | collective-permute-start | bytes 811016 | tf_op jit(solution)/shard_map/ppermute | solution.py:294
  32.6 6.3 %collective-permute-start.7 = (bf16[32,4224]{1,0:T(8,128)(2,1)S(1)}, bf16[32,4224]{1,0:T(8,128)(2,1)S(1)}, u32[]{:S(2)}, u32[]{:S(2)}) collective-permute-start(bf16[32,4224]{1,0:T(8,128)(2,1)S(1)} %collective-permute-done.5.refs_1_), channel_id=1, source_target_pairs={{0,1},{1,0},{2,3},{3,2},{4,5},{5,4},{6,7},{7,6},{8,9},{9,8},{10,11... | collective-permute-start | bytes 811016 | tf_op jit(solution)/shard_map/ppermute | solution.py:294
  38.7 7.5 %collective-permute-start.13 = (bf16[2,2,64,512]{3,2,1,0:T(8,128)(2,1)S(1)}, bf16[2,2,64,512]{3,2,1,0:T(8,128)(2,1)S(1)}, u32[]{:S(2)}, u32[]{:S(2)}) collective-permute-start(bf16[2,2,64,512]{3,2,1,0:T(8,128)(2,1)S(1)} %get-tuple-element.26), channel_id=1, source_target_pairs={{0,1},{1,0},{2,3},{3,2},{4,5},{5,4},{6,7},{7,6},{8,9},{9,8},{10,11... | collective-permute-start | bytes 786440 | tf_op jit(solution)/shard_map/ppermute | solution.py:294
  44.1 7.3 %collective-permute-start.11 = (bf16[2,2,64,512]{3,2,1,0:T(8,128)(2,1)S(1)}, bf16[2,2,64,512]{3,2,1,0:T(8,128)(2,1)S(1)}, u32[]{:S(2)}, u32[]{:S(2)}) collective-permute-start(bf16[2,2,64,512]{3,2,1,0:T(8,128)(2,1)S(1)} %get-tuple-element.23), channel_id=1, source_target_pairs={{0,1},{1,0},{2,3},{3,2},{4,5},{5,4},{6,7},{7,6},{8,9},{9,8},{10,11... | collective-permute-start | bytes 786440 | tf_op jit(solution)/shard_map/ppermute | solution.py:294
  46.3 10.8 %collective-permute-start.14 = (bf16[2,64,512]{2,1,0:T(8,128)(2,1)S(1)}, bf16[2,64,512]{2,1,0:T(8,128)(2,1)S(1)}, u32[]{:S(2)}, u32[]{:S(2)}) collective-permute-start(bf16[2,64,512]{2,1,0:T(8,128)(2,1)S(1)} %get-tuple-element.28), channel_id=1, source_target_pairs={{0,16},{8,24},{16,0},{24,8},{1,17},{9,25},{17,1},{25,9},{2,18},{10... | collective-permute-start | bytes 393224 | tf_op jit(solution)/shard_map/ppermute | solution.py:294
  51.4 9.1 %collective-permute-start.12 = (bf16[2,64,512]{2,1,0:T(8,128)(2,1)S(1)}, bf16[2,64,512]{2,1,0:T(8,128)(2,1)S(1)}, u32[]{:S(2)}, u32[]{:S(2)}) collective-permute-start(bf16[2,64,512]{2,1,0:T(8,128)(2,1)S(1)} %get-tuple-element.24), channel_id=1, source_target_pairs={{0,8},{8,0},{16,24},{24,16},{1,9},{9,1},{17,25},{25,17},{2,10},{10... | collective-permute-start | bytes 393224 | tf_op jit(solution)/shard_map/ppermute | solution.py:294
  51.6 10.6 %collective-permute-start.16 = (bf16[64,512]{1,0:T(8,128)(2,1)S(1)}, bf16[64,512]{1,0:T(8,128)(2,1)S(1)}, u32[]{:S(2)}, u32[]{:S(2)}) collective-permute-start(bf16[64,512]{1,0:T(8,128)(2,1)S(1)} %get-tuple-element.29), channel_id=1, source_target_pairs={{0,26},{1,29},{2,24},{3,31},{4,30},{5,25},{6,28},{7,27},{8,18},{9,... | collective-permute-start | bytes 196616 | tf_op jit(solution)/shard_map/ppermute | solution.py:305
  60.6 4.3 %collective-permute-start.15 = (bf16[64,512]{1,0:T(8,128)(2,1)S(1)}, bf16[64,512]{1,0:T(8,128)(2,1)S(1)}, u32[]{:S(2)}, u32[]{:S(2)}) collective-permute-start(bf16[64,512]{1,0:T(8,128)(2,1)S(1)} %get-tuple-element.37), channel_id=1, source_target_pairs={{0,2},{1,5},{2,0},{3,7},{4,6},{5,1},{6,4},{7,3},{8,10},{9,13},{10,... | collective-permute-start | bytes 196616 | tf_op jit(solution)/shard_map/ppermute | solution.py:305
  61.6 6.4 %collective-permute-start.18 = (bf16[64,512]{1,0:T(8,128)(2,1)S(1)}, bf16[64,512]{1,0:T(8,128)(2,1)S(1)}, u32[]{:S(2)}, u32[]{:S(2)}) collective-permute-start(bf16[64,512]{1,0:T(8,128)(2,1)S(1)} %get-tuple-element.30), channel_id=1, source_target_pairs={{0,24},{1,31},{2,26},{3,29},{4,28},{5,27},{6,30},{7,25},{8,16},{9,... | collective-permute-start | bytes 196616 | tf_op jit(solution)/shard_map/ppermute | solution.py:305
  61.6 6.4 %collective-permute-start.17 = (bf16[64,512]{1,0:T(8,128)(2,1)S(1)}, bf16[64,512]{1,0:T(8,128)(2,1)S(1)}, u32[]{:S(2)}, u32[]{:S(2)}) collective-permute-start(bf16[64,512]{1,0:T(8,128)(2,1)S(1)} %get-tuple-element.38), channel_id=1, source_target_pairs={{0,0},{1,7},{2,2},{3,5},{4,4},{5,3},{6,6},{7,1},{8,8},{9,15},{10,1... | collective-permute-start | bytes 196616 | tf_op jit(solution)/shard_map/ppermute | solution.py:305
  68.1 1.3 %collective-permute-start.19 = (bf16[64,512]{1,0:T(8,128)(2,1)S(1)}, bf16[64,512]{1,0:T(8,128)(2,1)S(1)}, u32[]{:S(2)}, u32[]{:S(2)}) collective-permute-start(bf16[64,512]{1,0:T(8,128)(2,1)S(1)} %pad_maximum_fusion.5), channel_id=1, source_target_pairs={{0,1},{1,0},{2,3},{3,2},{4,5},{5,4},{6,7},{7,6},{8,9},{9,8},{10,11... | collective-permute-start | bytes 196616 | tf_op jit(solution)/shard_map/ppermute | solution.py:294

commit v4 on v3

--- a/solution.py
+++ b/solution.py
@@ -182,11 +182,14 @@
     put_places(scalars, total, give_out)
 
 
+def even(index):
+    return 2 * index + bin(index).count("1") % 2
+
+
 def add_places(scalars, core, hidden, both_t, e, total):
     cols = total.shape[2]
-    groups = both_t.shape[2] // cols
     for index in range(total.shape[0]):
-        start = (scalars[0] ^ (core * (groups - 1)) ^ index) * cols
+        start = (scalars[0] ^ core ^ even(index)) * cols
         columns = pl.ds(pl.multiple_of(start, LANES), cols)
         term = jnp.dot(hidden, both_t[e, :, columns], preferred_element_type=jnp.float32)
         if e == 0:
@@ -300,7 +303,7 @@
     for w in range(wide_size):
         for g in range(groups):
             for r in range(2):
-                target = (w ^ wide_step) * groups + (g ^ (r * (groups - 1)) ^ index)
+                target = (w ^ wide_step) * groups + (g ^ r ^ even(index))
                 pairs.append(((w * groups + g) * 2 + r, target * 2 + r))
     return lax.ppermute(array, ("wide", "grp", "rep"), pairs)
 
@@ -390,9 +393,12 @@
         piece = piece.astype(jnp.bfloat16)
         keep.append(jnp.where(first_core, piece[:height], piece[height:]))
         give.append(jnp.where(first_core, piece[height:], piece[:height]))
-    taken = flip(jnp.concatenate(give[::-1], axis=0), "rep", 1)
-    pieces = keep + [taken[i * height : (i + 1) * height] for i in range(groups // 2)]
-    place = place ^ (rep * (groups - 1))
+    taken = flip(jnp.concatenate(give, axis=0), "rep", 1)
+    pieces = [None] * groups
+    for index in range(groups // 2):
+        pieces[even(index)] = keep[index]
+        pieces[even(index) ^ 1] = taken[index * height : (index + 1) * height]
+    place = place ^ rep
     bit = 1
     while bit < groups:
         swap = (place & bit) != 0

time: 70.3 us -> 72.2 us (1.027)
  waiting for transfers between devices: 27 us -> 28.6 us
    ppermute x4, waiting for transfers between devices: 5.72 us -> 6.97 us  [straight(): return lax.ppermute(array, ('wide', 'grp', 'rep'), pairs)]
  transfers between devices with their start and end apart: 20 -> 20, of which waited for: 8 -> 7; matrix products, arithmetic and copies ran while one was open for 2% -> 2% of each run, Pallas kernels for 30% -> 29%
where the time goes in v4:
time: 72.2 us; the launch traced here: 72 us
  waiting for transfers between devices  28.6 us (40%)
  Pallas kernels  21.2 us (29%)
  starting transfers between devices  19 us (26%)
  local copies, waits for them, and re-layouts  2.05 us (3%)
  other arithmetic  0.93 us (1%)
    ppermute x16, waiting for transfers between devices, flip(): return lax.ppermute(array, axis, [(i, i ^ step) for i in range(size)])  21.6 us
    ppermute x16, starting transfers between devices, flip(): return lax.ppermute(array, axis, [(i, i ^ step) for i in range(size)])  15.4 us
    pallas_call x2, Pallas kernels, chunk_gradient(): pl.pallas_call(lambda *refs: chunk_kernel(groups, 2 * slots, turn, *refs)...  10.8 us
    pallas_call x1, Pallas kernels, load_weights(): pl.pallas_call(load_kernel, in_specs=[HBM] * 3 + [VMEM, SMEM], out_specs=...  7.07 us
    ppermute x4, waiting for transfers between devices, straight(): return lax.ppermute(array, ('wide', 'grp', 'rep'), pairs)  6.97 us
    ppermute x4, starting transfers between devices, straight(): return lax.ppermute(array, ('wide', 'grp', 'rep'), pairs)  3.62 us
    pallas_call x2, Pallas kernels, keep_gradient(): pl.pallas_call(keep_kernel, in_specs=[SMEM] + [VMEM] * 2, out_specs=VMEM,...  3.19 us
  transfers between devices with their start and end apart: 20, of which 7 were waited for; matrix products, arithmetic and copies ran while one was open for 2% of the time, Pallas kernels for 29%

profile of v4, /device:TPU:0, one launch (start us, length us, event | category | flops | bytes accessed | tf_op | source)
XLA Modules:
  0.0 72.0 jit_solution(11371572156912566343)
XLA Ops:
  0.0 0.0 copy-start
  0.0 0.9 %constant_dynamic-slice_fusion.2 = (bf16[32,512]{1,0:T(8,128)(2,1)S(1)}, bf16[32,512]{1,0:T(8,128)(2,1)S(1)}, bf16[32,512]{1,0:T(8,128)(2,1)S(1)}, bf16[32,512]{...) fusion(bf16[128,512]{1,0:T(8,128)(2,1)} %param.8, ...), kind=kLoop, calls=%fused_computation.31 | loop fusion | bytes 524304 | tf_op jit(solution)/shard_map/dynamic_slice | solution.py:342
  0.9 3.0 %collective-permute-start.1 = (bf16[32,1024]{1,0:T(8,128)(2,1)S(1)}, bf16[32,1024]{1,0:T(8,128)(2,1)S(1)}, u32[]{:S(2)}, u32[]{:S(2)}) collective-permute-start(bf16[32,1024]{1,0:T(8,128)(2,1)S(1)} %pad_maximum_fusion.2), channel_id=1, source_target_pairs={{0,2},{2,0},{4,6},{6,4},{1,3},{3,1},{5,7},{7,5},{8,10},{10,8},{12,... | collective-permute-start | bytes 196616 | tf_op jit(solution)/shard_map/ppermute | solution.py:297
  4.0 1.5 %collective-permute-start.2 = (bf16[32,1024]{1,0:T(8,128)(2,1)S(1)}, bf16[32,1024]{1,0:T(8,128)(2,1)S(1)}, u32[]{:S(2)}, u32[]{:S(2)}) collective-permute-start(bf16[32,1024]{1,0:T(8,128)(2,1)S(1)} %pad_maximum_fusion.3), channel_id=1, source_target_pairs={{0,4},{2,6},{4,0},{6,2},{1,5},{3,7},{5,1},{7,3},{8,12},{10,14},{12... | collective-permute-start | bytes 196616 | tf_op jit(solution)/shard_map/ppermute | solution.py:297
  5.5 0.1 collective-permute-start.3
  5.5 0.0 copy-done
  5.5 0.1 constant_dynamic-slice_fusion
  5.6 0.8 %constant_dynamic-slice_fusion.1 = s32[32,8]{0,1:T(8,128)S(1)} fusion(s32[128,8]{0,1:T(8,128)} %param.9, s32[]{:T(128)S(6)} %select_n.81), kind=kLoop, calls=%fused_computation.30 | loop fusion | bytes 2052 | tf_op jit(solution)/shard_map/dynamic_slice | solution.py:347
  6.4 0.1 copy.10
  6.5 0.0 collective-permute-done.1
  6.5 1.7 %collective-permute-done.2 = bf16[32,1024]{1,0:T(8,128)(2,1)S(1)} collective-permute-done((bf16[32,1024]{1,0:T(8,128)(2,1)S(1)}, bf16[32,1024]{1,0:T(8,128)(2,1)S(1)}, u32[]{:S(2)}, u32[]{:S(2)}) %collective-permute-start.2) | collective-permute-done | bytes 65568 | tf_op jit(solution)/shard_map/ppermute | solution.py:297
  8.2 2.4 %collective-permute-done.3 = bf16[32,1024]{1,0:T(8,128)(2,1)S(1)} collective-permute-done((bf16[32,1024]{1,0:T(8,128)(2,1)S(1)}, bf16[32,1024]{1,0:T(8,128)(2,1)S(1)}, u32[]{:S(2)}, u32[]{:S(2)}) %collective-permute-start.3) | collective-permute-done | bytes 65568 | tf_op jit(solution)/shard_map/ppermute | solution.py:297
  10.7 0.1 concatenate.32
  10.7 2.6 %collective-permute-start.4 = (bf16[32,3200]{1,0:T(8,128)(2,1)S(1)}, bf16[32,3200]{1,0:T(8,128)(2,1)S(1)}, u32[]{:S(2)}, u32[]{:S(2)}) collective-permute-start(bf16[32,3200]{1,0:T(8,128)(2,1)S(1)} %concatenate.32), channel_id=1, source_target_pairs={{0,16},{8,24},{16,0},{24,8},{1,17},{9,25},{17,1},{25,9},{2,18},{10... | collective-permute-start | bytes 614408 | tf_op jit(solution)/shard_map/ppermute | solution.py:297
  13.4 0.3 collective-permute-start
  13.7 0.1 concatenate.34.after.refs_2_
  13.8 1.6 %collective-permute-start.6 = (bf16[32,4224]{1,0:T(8,128)(2,1)S(1)}, bf16[32,4224]{1,0:T(8,128)(2,1)S(1)}, u32[]{:S(2)}, u32[]{:S(2)}) collective-permute-start(bf16[32,4224]{1,0:T(8,128)(2,1)S(1)} %concatenate.34.after.refs_2_), channel_id=1, source_target_pairs={{0,8},{8,0},{16,24},{24,16},{1,9},{9,1},{17,25},{25,17},{2,10},{10... | collective-permute-start | bytes 811016 | tf_op jit(solution)/shard_map/ppermute | solution.py:297
  15.5 8.6 %collective-permute-done = bf16[32,1024]{1,0:T(8,128)(2,1)S(1)} collective-permute-done((bf16[32,1024]{1,0:T(8,128)(2,1)S(1)}, bf16[32,1024]{1,0:T(8,128)(2,1)S(1)}, u32[]{:S(2)}, u32[]{:S(2)}) %collective-permute-start) | collective-permute-done | bytes 65568 | tf_op jit(solution)/shard_map/ppermute | solution.py:297
  24.1 0.0 collective-permute-done.4
  24.1 0.7 collective-permute-start.5
  24.8 0.0 collective-permute-start.10
  24.8 0.5 collective-permute-start.9
  25.3 0.1 pad_add_fusion.scalars.refs_0_
  25.4 7.1 %load.1 = (bf16[4,2048,768]{2,1,0:T(8,128)(2,1)S(1)}, bf16[4,768,2048]{2,1,0:T(8,128)(2,1)S(1)}, bf16[1536,2048]{1,0:T(8,128)(2,1)S(1)}) custom-call(bf16[4,2048,384]{2,1,0:T(8,128)(2,1)} %gate_hbm.1, bf16[4,2048,384]{2,1,0:T(8,128)(2,1)} %up_hbm.1, bf16[4,384,2048]{2,1,0:T(8,128)(2,1)} %down_hbm.1, bf16[32,4224]{1,0:T(8,128)(2,1)S(1)} %concatenate.34.after.refs_2_, ...), custom_call_target="tpu_custom_call" | custom-call | bytes 18874368 | tf_op jit(solution)/shard_map/load/pallas_call | solution.py:123
  32.5 0.0 collective-permute-done.6.refs_2_
  32.5 0.1 collective-permute-start.8
  32.6 0.0 collective-permute-done.5.refs_1_
  32.6 0.5 collective-permute-start.7
  33.1 0.0 collective-permute-done.10.refs_4_
  33.1 0.0 collective-permute-done.9.refs_3_
  33.1 5.6 %chunk.2 = (bf16[4,128,768]{2,1,0:T(8,128)(2,1)S(1)}, bf16[2,2,64,512]{3,2,1,0:T(8,128)(2,1)S(1)}, bf16[2048,1536]{1,0:T(8,128)(2,1)S(1)}) custom-call(s32[3]{0:T(128)S(1)} %pad_add_fusion.scalars.refs_0_, bf16[32,4224]{1,0:T(8,128)(2,1)S(1)} %constant_dynamic-update-slice_fusion.refs_1_, bf16[32,4224]{1,0:T(8,128)(2,1)S(1)} %concatenate.34.after.refs_2_, ...), custom_call_target="tpu_custom_call" | custom-call | flops 4026531840 | bytes 1048576 | tf_op jit(solution)/shard_map/chunk/pallas_call | solution.py:242
  38.7 0.2 collective-permute-start.13
  38.9 0.0 collective-permute-done.8.refs_4_
  38.9 0.0 collective-permute-done.7.refs_3_
  38.9 5.2 %chunk.3 = (bf16[4,128,768]{2,1,0:T(8,128)(2,1)S(1)}, bf16[2,2,64,512]{3,2,1,0:T(8,128)(2,1)S(1)}) custom-call(s32[3]{0:T(128)S(1)} %pad_add_fusion.scalars.refs_0_, bf16[32,4224]{1,0:T(8,128)(2,1)S(1)} %collective-permute-done.5.refs_1_, bf16[32,4224]{1,0:T(8,128)(2,1)S(1)} %collective-permute-done.6.refs_2_, ...), custom_call_target="tpu_custom_call" | custom-call | flops 4026531840 | bytes 1048576 | tf_op jit(solution)/shard_map/chunk/pallas_call | solution.py:242
  44.1 0.5 collective-permute-start.11
  44.6 1.6 %keep.3.refs_0_ = f32[2,2,64,512]{3,2,1,0:T(8,128)S(1)} custom-call(s32[3]{0:T(128)S(1)} %pad_add_fusion.scalars.refs_0_, bf16[4,128,768]{2,1,0:T(8,128)(2,1)S(1)} %get-tuple-element.25.hidden, bf16[4,768,2048]{2,1,0:T(8,128)(2,1)S(1)} %get-tuple-element.19.refs_6_.both_t), custom_call_target="tpu_custom_call" | custom-call | flops 805306368 | bytes 786432 | tf_op jit(solution)/shard_map/keep/pallas_call | solution.py:221
  46.2 0.0 collective-permute-done.13.refs_1_
  46.3 3.5 %collective-permute-start.14 = (bf16[2,64,512]{2,1,0:T(8,128)(2,1)S(1)}, bf16[2,64,512]{2,1,0:T(8,128)(2,1)S(1)}, u32[]{:S(2)}, u32[]{:S(2)}) collective-permute-start(bf16[2,64,512]{2,1,0:T(8,128)(2,1)S(1)} %get-tuple-element.28), channel_id=1, source_target_pairs={{0,16},{8,24},{16,0},{24,8},{1,17},{9,25},{17,1},{25,9},{2,18},{10... | collective-permute-start | bytes 393224 | tf_op jit(solution)/shard_map/ppermute | solution.py:297
  49.8 1.6 %keep.2.refs_0_ = f32[2,2,64,512]{3,2,1,0:T(8,128)S(1)} custom-call(s32[3]{0:T(128)S(1)} %pad_add_fusion.scalars.refs_0_, bf16[4,128,768]{2,1,0:T(8,128)(2,1)S(1)} %get-tuple-element.22.hidden, bf16[4,768,2048]{2,1,0:T(8,128)(2,1)S(1)} %get-tuple-element.19.refs_6_.both_t), custom_call_target="tpu_custom_call" | custom-call | flops 805306368 | bytes 786432 | tf_op jit(solution)/shard_map/keep/pallas_call | solution.py:221
  51.4 0.0 collective-permute-done.11.refs_1_
  51.4 0.2 collective-permute-start.12
  51.6 1.4 %collective-permute-start.18 = (bf16[64,512]{1,0:T(8,128)(2,1)S(1)}, bf16[64,512]{1,0:T(8,128)(2,1)S(1)}, u32[]{:S(2)}, u32[]{:S(2)}) collective-permute-start(bf16[64,512]{1,0:T(8,128)(2,1)S(1)} %get-tuple-element.30), channel_id=1, source_target_pairs={{0,24},{1,27},{2,26},{3,25},{4,28},{5,31},{6,30},{7,29},{8,16},{9,... | collective-permute-start | bytes 196616 | tf_op jit(solution)/shard_map/ppermute | solution.py:308
  53.0 3.8 %collective-permute-done.14 = bf16[2,64,512]{2,1,0:T(8,128)(2,1)S(1)} collective-permute-done((bf16[2,64,512]{2,1,0:T(8,128)(2,1)S(1)}, bf16[2,64,512]{2,1,0:T(8,128)(2,1)S(1)}, u32[]{:S(2)}, u32[]{:S(2)}) %collective-permute-start.14) | collective-permute-done | bytes 131104 | tf_op jit(solution)/shard_map/ppermute | solution.py:297
  56.7 3.8 %collective-permute-done.12 = bf16[2,64,512]{2,1,0:T(8,128)(2,1)S(1)} collective-permute-done((bf16[2,64,512]{2,1,0:T(8,128)(2,1)S(1)}, bf16[2,64,512]{2,1,0:T(8,128)(2,1)S(1)}, u32[]{:S(2)}, u32[]{:S(2)}) %collective-permute-start.12) | collective-permute-done | bytes 131104 | tf_op jit(solution)/shard_map/ppermute | solution.py:297
  60.6 0.7 collective-permute-start.17
  61.3 0.1 collective-permute-start.16
  61.4 1.5 %collective-permute-start.15 = (bf16[64,512]{1,0:T(8,128)(2,1)S(1)}, bf16[64,512]{1,0:T(8,128)(2,1)S(1)}, u32[]{:S(2)}, u32[]{:S(2)}) collective-permute-start(bf16[64,512]{1,0:T(8,128)(2,1)S(1)} %get-tuple-element.38), channel_id=1, source_target_pairs={{0,6},{1,5},{2,4},{3,7},{4,2},{5,1},{6,0},{7,3},{8,14},{9,13},{10,... | collective-permute-start | bytes 196616 | tf_op jit(solution)/shard_map/ppermute | solution.py:308
  62.9 0.0 collective-permute-done.18
  62.9 0.0 collective-permute-done.17
  63.0 7.0 %collective-permute-done.16 = bf16[64,512]{1,0:T(8,128)(2,1)S(1)} collective-permute-done((bf16[64,512]{1,0:T(8,128)(2,1)S(1)}, bf16[64,512]{1,0:T(8,128)(2,1)S(1)}, u32[]{:S(2)}, u32[]{:S(2)}) %collective-permute-start.16) | collective-permute-done | bytes 65568 | tf_op jit(solution)/shard_map/ppermute | solution.py:308
  69.9 0.0 collective-permute-done.15
  70.0 0.1 collective-permute-start.19
  70.1 1.2 %collective-permute-done.19 = bf16[64,512]{1,0:T(8,128)(2,1)S(1)} collective-permute-done((bf16[64,512]{1,0:T(8,128)(2,1)S(1)}, bf16[64,512]{1,0:T(8,128)(2,1)S(1)}, u32[]{:S(2)}, u32[]{:S(2)}) %collective-permute-start.19) | collective-permute-done | bytes 65568 | tf_op jit(solution)/shard_map/ppermute | solution.py:297
  71.3 0.7 pad_maximum_fusion
  (20 shorter events, 0.3 us)
Async XLA Ops:
  0.0 5.5 %copy-start = (f32[128,8]{0,1:T(8,128)S(1)}, f32[128,8]{0,1:T(8,128)}, u32[]{:S(2)}) copy-start(f32[128,8]{0,1:T(8,128)} %param.10) | copy-start | bytes 12292
  0.9 5.6 %collective-permute-start.1 = (bf16[32,1024]{1,0:T(8,128)(2,1)S(1)}, bf16[32,1024]{1,0:T(8,128)(2,1)S(1)}, u32[]{:S(2)}, u32[]{:S(2)}) collective-permute-start(bf16[32,1024]{1,0:T(8,128)(2,1)S(1)} %pad_maximum_fusion.2), channel_id=1, source_target_pairs={{0,2},{2,0},{4,6},{6,4},{1,3},{3,1},{5,7},{7,5},{8,10},{10,8},{12,... | collective-permute-start | bytes 196616 | tf_op jit(solution)/shard_map/ppermute | solution.py:297
  4.0 4.3 %collective-permute-start.2 = (bf16[32,1024]{1,0:T(8,128)(2,1)S(1)}, bf16[32,1024]{1,0:T(8,128)(2,1)S(1)}, u32[]{:S(2)}, u32[]{:S(2)}) collective-permute-start(bf16[32,1024]{1,0:T(8,128)(2,1)S(1)} %pad_maximum_fusion.3), channel_id=1, source_target_pairs={{0,4},{2,6},{4,0},{6,2},{1,5},{3,7},{5,1},{7,3},{8,12},{10,14},{12... | collective-permute-start | bytes 196616 | tf_op jit(solution)/shard_map/ppermute | solution.py:297
  5.5 5.2 %collective-permute-start.3 = (bf16[32,1024]{1,0:T(8,128)(2,1)S(1)}, bf16[32,1024]{1,0:T(8,128)(2,1)S(1)}, u32[]{:S(2)}, u32[]{:S(2)}) collective-permute-start(bf16[32,1024]{1,0:T(8,128)(2,1)S(1)} %pad_maximum_fusion.4), channel_id=1, source_target_pairs={{0,6},{2,4},{4,2},{6,0},{1,7},{3,5},{5,3},{7,1},{8,14},{10,12},{12... | collective-permute-start | bytes 196616 | tf_op jit(solution)/shard_map/ppermute | solution.py:297
  10.7 13.4 %collective-permute-start.4 = (bf16[32,3200]{1,0:T(8,128)(2,1)S(1)}, bf16[32,3200]{1,0:T(8,128)(2,1)S(1)}, u32[]{:S(2)}, u32[]{:S(2)}) collective-permute-start(bf16[32,3200]{1,0:T(8,128)(2,1)S(1)} %concatenate.32), channel_id=1, source_target_pairs={{0,16},{8,24},{16,0},{24,8},{1,17},{9,25},{17,1},{25,9},{2,18},{10... | collective-permute-start | bytes 614408 | tf_op jit(solution)/shard_map/ppermute | solution.py:297
  13.4 10.7 %collective-permute-start = (bf16[32,1024]{1,0:T(8,128)(2,1)S(1)}, bf16[32,1024]{1,0:T(8,128)(2,1)S(1)}, u32[]{:S(2)}, u32[]{:S(2)}) collective-permute-start(bf16[32,1024]{1,0:T(8,128)(2,1)S(1)} %pad_maximum_fusion.1), channel_id=1, source_target_pairs={{0,16},{8,24},{16,0},{24,8},{1,17},{9,25},{17,1},{25,9},{2,18},{10... | collective-permute-start | bytes 196616 | tf_op jit(solution)/shard_map/ppermute | solution.py:297
  13.8 18.7 %collective-permute-start.6 = (bf16[32,4224]{1,0:T(8,128)(2,1)S(1)}, bf16[32,4224]{1,0:T(8,128)(2,1)S(1)}, u32[]{:S(2)}, u32[]{:S(2)}) collective-permute-start(bf16[32,4224]{1,0:T(8,128)(2,1)S(1)} %concatenate.34.after.refs_2_), channel_id=1, source_target_pairs={{0,8},{8,0},{16,24},{24,16},{1,9},{9,1},{17,25},{25,17},{2,10},{10... | collective-permute-start | bytes 811016 | tf_op jit(solution)/shard_map/ppermute | solution.py:297
  24.1 8.4 %collective-permute-start.5 = (bf16[32,4224]{1,0:T(8,128)(2,1)S(1)}, bf16[32,4224]{1,0:T(8,128)(2,1)S(1)}, u32[]{:S(2)}, u32[]{:S(2)}) collective-permute-start(bf16[32,4224]{1,0:T(8,128)(2,1)S(1)} %constant_dynamic-update-slice_fusion.refs_1_), channel_id=1, source_target_pairs={{0,8},{8,0},{16,24},{24,16},{1,9},{9,1},{17,25},{25,17},{2,10},{10... | collective-permute-start | bytes 811016 | tf_op jit(solution)/shard_map/ppermute | solution.py:297
  24.8 8.3 %collective-permute-start.10 = (bf16[32,4224]{1,0:T(8,128)(2,1)S(1)}, bf16[32,4224]{1,0:T(8,128)(2,1)S(1)}, u32[]{:S(2)}, u32[]{:S(2)}) collective-permute-start(bf16[32,4224]{1,0:T(8,128)(2,1)S(1)} %concatenate.34.after.refs_2_), channel_id=1, source_target_pairs={{0,1},{1,0},{2,3},{3,2},{4,5},{5,4},{6,7},{7,6},{8,9},{9,8},{10,11... | collective-permute-start | bytes 811016 | tf_op jit(solution)/shard_map/ppermute | solution.py:297
  24.8 8.3 %collective-permute-start.9 = (bf16[32,4224]{1,0:T(8,128)(2,1)S(1)}, bf16[32,4224]{1,0:T(8,128)(2,1)S(1)}, u32[]{:S(2)}, u32[]{:S(2)}) collective-permute-start(bf16[32,4224]{1,0:T(8,128)(2,1)S(1)} %constant_dynamic-update-slice_fusion.refs_1_), channel_id=1, source_target_pairs={{0,1},{1,0},{2,3},{3,2},{4,5},{5,4},{6,7},{7,6},{8,9},{9,8},{10,11... | collective-permute-start | bytes 811016 | tf_op jit(solution)/shard_map/ppermute | solution.py:297
  32.5 6.4 %collective-permute-start.8 = (bf16[32,4224]{1,0:T(8,128)(2,1)S(1)}, bf16[32,4224]{1,0:T(8,128)(2,1)S(1)}, u32[]{:S(2)}, u32[]{:S(2)}) collective-permute-start(bf16[32,4224]{1,0:T(8,128)(2,1)S(1)} %collective-permute-done.6.refs_2_), channel_id=1, source_target_pairs={{0,1},{1,0},{2,3},{3,2},{4,5},{5,4},{6,7},{7,6},{8,9},{9,8},{10,11... | collective-permute-start | bytes 811016 | tf_op jit(solution)/shard_map/ppermute | solution.py:297
  32.6 6.3 %collective-permute-start.7 = (bf16[32,4224]{1,0:T(8,128)(2,1)S(1)}, bf16[32,4224]{1,0:T(8,128)(2,1)S(1)}, u32[]{:S(2)}, u32[]{:S(2)}) collective-permute-start(bf16[32,4224]{1,0:T(8,128)(2,1)S(1)} %collective-permute-done.5.refs_1_), channel_id=1, source_target_pairs={{0,1},{1,0},{2,3},{3,2},{4,5},{5,4},{6,7},{7,6},{8,9},{9,8},{10,11... | collective-permute-start | bytes 811016 | tf_op jit(solution)/shard_map/ppermute | solution.py:297
  38.7 7.5 %collective-permute-start.13 = (bf16[2,2,64,512]{3,2,1,0:T(8,128)(2,1)S(1)}, bf16[2,2,64,512]{3,2,1,0:T(8,128)(2,1)S(1)}, u32[]{:S(2)}, u32[]{:S(2)}) collective-permute-start(bf16[2,2,64,512]{3,2,1,0:T(8,128)(2,1)S(1)} %get-tuple-element.26), channel_id=1, source_target_pairs={{0,1},{1,0},{2,3},{3,2},{4,5},{5,4},{6,7},{7,6},{8,9},{9,8},{10,11... | collective-permute-start | bytes 786440 | tf_op jit(solution)/shard_map/ppermute | solution.py:297
  44.1 7.3 %collective-permute-start.11 = (bf16[2,2,64,512]{3,2,1,0:T(8,128)(2,1)S(1)}, bf16[2,2,64,512]{3,2,1,0:T(8,128)(2,1)S(1)}, u32[]{:S(2)}, u32[]{:S(2)}) collective-permute-start(bf16[2,2,64,512]{3,2,1,0:T(8,128)(2,1)S(1)} %get-tuple-element.23), channel_id=1, source_target_pairs={{0,1},{1,0},{2,3},{3,2},{4,5},{5,4},{6,7},{7,6},{8,9},{9,8},{10,11... | collective-permute-start | bytes 786440 | tf_op jit(solution)/shard_map/ppermute | solution.py:297
  46.3 10.5 %collective-permute-start.14 = (bf16[2,64,512]{2,1,0:T(8,128)(2,1)S(1)}, bf16[2,64,512]{2,1,0:T(8,128)(2,1)S(1)}, u32[]{:S(2)}, u32[]{:S(2)}) collective-permute-start(bf16[2,64,512]{2,1,0:T(8,128)(2,1)S(1)} %get-tuple-element.28), channel_id=1, source_target_pairs={{0,16},{8,24},{16,0},{24,8},{1,17},{9,25},{17,1},{25,9},{2,18},{10... | collective-permute-start | bytes 393224 | tf_op jit(solution)/shard_map/ppermute | solution.py:297
  51.4 9.1 %collective-permute-start.12 = (bf16[2,64,512]{2,1,0:T(8,128)(2,1)S(1)}, bf16[2,64,512]{2,1,0:T(8,128)(2,1)S(1)}, u32[]{:S(2)}, u32[]{:S(2)}) collective-permute-start(bf16[2,64,512]{2,1,0:T(8,128)(2,1)S(1)} %get-tuple-element.24), channel_id=1, source_target_pairs={{0,8},{8,0},{16,24},{24,16},{1,9},{9,1},{17,25},{25,17},{2,10},{10... | collective-permute-start | bytes 393224 | tf_op jit(solution)/shard_map/ppermute | solution.py:297
  51.6 11.3 %collective-permute-start.18 = (bf16[64,512]{1,0:T(8,128)(2,1)S(1)}, bf16[64,512]{1,0:T(8,128)(2,1)S(1)}, u32[]{:S(2)}, u32[]{:S(2)}) collective-permute-start(bf16[64,512]{1,0:T(8,128)(2,1)S(1)} %get-tuple-element.30), channel_id=1, source_target_pairs={{0,24},{1,27},{2,26},{3,25},{4,28},{5,31},{6,30},{7,29},{8,16},{9,... | collective-permute-start | bytes 196616 | tf_op jit(solution)/shard_map/ppermute | solution.py:308
  60.6 2.3 %collective-permute-start.17 = (bf16[64,512]{1,0:T(8,128)(2,1)S(1)}, bf16[64,512]{1,0:T(8,128)(2,1)S(1)}, u32[]{:S(2)}, u32[]{:S(2)}) collective-permute-start(bf16[64,512]{1,0:T(8,128)(2,1)S(1)} %get-tuple-element.37), channel_id=1, source_target_pairs={{0,0},{1,3},{2,2},{3,1},{4,4},{5,7},{6,6},{7,5},{8,8},{9,11},{10,1... | collective-permute-start | bytes 196616 | tf_op jit(solution)/shard_map/ppermute | solution.py:308
  61.3 8.6 %collective-permute-start.16 = (bf16[64,512]{1,0:T(8,128)(2,1)S(1)}, bf16[64,512]{1,0:T(8,128)(2,1)S(1)}, u32[]{:S(2)}, u32[]{:S(2)}) collective-permute-start(bf16[64,512]{1,0:T(8,128)(2,1)S(1)} %get-tuple-element.29), channel_id=1, source_target_pairs={{0,30},{1,29},{2,28},{3,31},{4,26},{5,25},{6,24},{7,27},{8,22},{9,... | collective-permute-start | bytes 196616 | tf_op jit(solution)/shard_map/ppermute | solution.py:308
  61.4 8.5 %collective-permute-start.15 = (bf16[64,512]{1,0:T(8,128)(2,1)S(1)}, bf16[64,512]{1,0:T(8,128)(2,1)S(1)}, u32[]{:S(2)}, u32[]{:S(2)}) collective-permute-start(bf16[64,512]{1,0:T(8,128)(2,1)S(1)} %get-tuple-element.38), channel_id=1, source_target_pairs={{0,6},{1,5},{2,4},{3,7},{4,2},{5,1},{6,0},{7,3},{8,14},{9,13},{10,... | collective-permute-start | bytes 196616 | tf_op jit(solution)/shard_map/ppermute | solution.py:308
  70.0 1.3 %collective-permute-start.19 = (bf16[64,512]{1,0:T(8,128)(2,1)S(1)}, bf16[64,512]{1,0:T(8,128)(2,1)S(1)}, u32[]{:S(2)}, u32[]{:S(2)}) collective-permute-start(bf16[64,512]{1,0:T(8,128)(2,1)S(1)} %pad_maximum_fusion.5), channel_id=1, source_target_pairs={{0,1},{1,0},{2,3},{3,2},{4,5},{5,4},{6,7},{7,6},{8,9},{9,8},{10,11... | collective-permute-start | bytes 196616 | tf_op jit(solution)/shard_map/ppermute | solution.py:297
